TPU v7x, 256 devices: a whole 4x4x8 slice. The times are simulated.
256 devices in a mesh: blk: 8 (over y_hi, x), head: 8 (over z), bend: 4 (over y_lo, core).
Axes of the slice: x: 4, y: 4 (y_hi: 2, y_lo: 2; y = y_hi * 2 + y_lo), z: 8, core: 2. Of those that a mesh axis runs over, the one named last changes fastest.
Arguments:
- queries: bfloat16 [65536, 768], P(('bend', 'blk', 'head')), parts along dimension 0, may hold values from -9 to 9
- keys_values: bfloat16 [2, 65536, 768], P(None, ('bend', 'blk', 'head')), parts along dimension 1, may hold values from -6 to 6
- surface: bfloat16 [65536, 768], P(('bend', 'blk', 'head')), parts along dimension 0, may hold values from -6 to 6
- out_weight: bfloat16 [768, 768], P('head'), may hold values from -0.21875 to 0.21875
- up_weight: bfloat16 [768, 3072], P('head'), may hold values from -0.21875 to 0.21875
- down_weight: bfloat16 [3072, 768], P('head'), may hold values from -0.109375 to 0.109375
- norm_gain: float32 [768], replicated, may hold values from 0.25 to 1.75
- block_lists: int32 [256, 4], P(('bend', 'blk', 'head')), parts along dimension 0, may hold values from 0 to 63, as said below
- list_lengths: int32 [256], P(('bend', 'blk', 'head')), parts along dimension 0, may hold values from 1 to 4
Outputs:
- mixed_out: bfloat16 [65536, 768], P(('bend', 'blk', 'head')), parts along dimension 0
There are 4 independent parts, one for each index of `bend`. A program takes and returns all parts, laid end to end along the dimension named above; an argument that names none is the same for every part. Nothing has to cross between parts.
Inputs may be any that keep to these rules, and one draw needn't show every extreme that they name: `block_lists`: the list of query block b holds distinct anchor blocks, all within cycle distance 3 (modulo 64) of anchor block b, and its first entry is that block itself.
All inputs are finite; a program needn't handle non-finite values.
Results may differ from a plain program's by a relative error of at most 0.0065.
Values may be sent and summed in bfloat16 or wider, within the bound.
A program may use at most 128 MiB of HBM per device.

v0:
```python
import functools

import jax
import jax.numpy as jnp
from jax import lax
from jax.experimental import pallas as pl
from jax.experimental.pallas import tpu as pltpu
from jax.sharding import PartitionSpec as P

HEADS = 12
HD = 64
LIST = 4
REACH = 3


def ring_shift(block, axis, size, distance):
    route = [(i, (i + distance) % size) for i in range(size)]
    return lax.ppermute(block, axis, route)


def x_shift(block, blk_size, x_size, distance):
    route = []
    for i in range(blk_size):
        hi, x = divmod(i, x_size)
        route.append((i, hi * x_size + (x + distance) % x_size))
    return lax.ppermute(block, "blk", route)


def core_swap(block, bend_size):
    route = [(i, i ^ 1) for i in range(bend_size)]
    return lax.ppermute(block, "bend", route)


def attention_kernel(n_blocks, mask_ref, q_ref, *refs):
    kv_refs = refs[:n_blocks]
    o_ref = refs[n_blocks]
    m_scr, l_scr, acc_scr = refs[n_blocks + 1:]
    scale = 1.0 / HD**0.5
    q_t = q_ref[...].T
    first = lax.broadcasted_iota(jnp.int32, q_t.shape, 0) < HD
    zero = jnp.zeros_like(q_t)
    halves = (jnp.where(first, q_t, zero), jnp.where(first, zero, q_t))
    for hh in range(2):
        m_scr[hh] = jnp.full(m_scr.shape[1:], -jnp.inf, jnp.float32)
        l_scr[hh] = jnp.zeros(l_scr.shape[1:], jnp.float32)
        acc_scr[hh] = jnp.zeros(acc_scr.shape[1:], jnp.float32)
    for j in range(n_blocks):
        @pl.when(mask_ref[j] > 0)
        def _():
            k = kv_refs[j][0]
            for hh in range(2):
                s_t = jnp.dot(k, halves[hh], preferred_element_type=jnp.float32) * scale
                m_scr[hh] = jnp.maximum(m_scr[hh], jnp.max(s_t, axis=0, keepdims=True))
    for j in range(n_blocks):
        @pl.when(mask_ref[j] > 0)
        def _():
            k = kv_refs[j][0]
            v_t = kv_refs[j][1].T
            for hh in range(2):
                s_t = jnp.dot(k, halves[hh], preferred_element_type=jnp.float32) * scale
                w_t = jnp.exp(s_t - m_scr[hh])
                l_scr[hh] += jnp.sum(w_t, axis=0, keepdims=True)
                acc_scr[hh] += jnp.dot(v_t, w_t.astype(jnp.bfloat16),
                                       preferred_element_type=jnp.float32)
    lane = lax.broadcasted_iota(jnp.int32, acc_scr.shape[1:], 0) < HD
    out_t = jnp.where(lane, acc_scr[0] / l_scr[0], acc_scr[1] / l_scr[1])
    o_ref[...] = out_t.T.astype(o_ref.dtype)


def attend(mask, q, blocks):
    rows, width = q.shape
    n_blocks = len(blocks)
    pair = 2 * HD
    grid_spec = pltpu.PrefetchScalarGridSpec(
        num_scalar_prefetch=1,
        grid=(width // pair,),
        in_specs=[pl.BlockSpec((rows, pair), lambda p, m: (0, p))]
        + [pl.BlockSpec((2, rows, pair), lambda p, m: (0, 0, p))] * n_blocks,
        out_specs=pl.BlockSpec((rows, pair), lambda p, m: (0, p)),
        scratch_shapes=[
            pltpu.VMEM((2, 1, rows), jnp.float32),
            pltpu.VMEM((2, 1, rows), jnp.float32),
            pltpu.VMEM((2, pair, rows), jnp.float32),
        ],
    )
    return pl.pallas_call(
        functools.partial(attention_kernel, n_blocks),
        grid_spec=grid_spec,
        out_shape=jax.ShapeDtypeStruct((rows, width), jnp.bfloat16),
        cost_estimate=pl.CostEstimate(
            flops=12 * rows * rows * width * 4,
            transcendentals=rows * rows * HEADS * 4,
            bytes_accessed=2 * rows * width * (2 * n_blocks + 2),
        ),
    )(mask, q, *blocks)


def order_of(offsets, me, n):
    held = (me + jnp.array(offsets, jnp.int32)) % n
    return jnp.argmax(held[None, :] == jnp.arange(n, dtype=jnp.int32)[:, None], axis=1)


def split_halves(tree, take_first):
    return tuple(w[: w.shape[0] // 2] if take_first else w[w.shape[0] // 2:] for w in tree)


def gather_over_head(pieces, n):
    me = lax.axis_index("head")
    rel, offsets = [pieces], [0]
    left = right = pieces
    for k in range(1, n // 2):
        left = ring_shift(left, "head", n, 1)
        right = ring_shift(right, "head", n, -1)
        rel += [left, right]
        offsets += [-k, k]
    far_top = ring_shift(split_halves(left, True), "head", n, 1)
    far_bottom = ring_shift(split_halves(right, False), "head", n, -1)
    rel.append(tuple(jnp.concatenate([a, b], axis=0) for a, b in zip(far_top, far_bottom)))
    offsets.append(n // 2)
    order = order_of(offsets, me, n)
    return tuple(jnp.take(jnp.stack([r[k] for r in rel]), order, axis=0)
                 for k in range(len(pieces)))


def gather_over_x_and_core(pieces, blk_size, x_size, bend_size, x, core):
    from_left = x_shift(pieces, blk_size, x_size, 1)
    from_right = x_shift(pieces, blk_size, x_size, -1)
    far_top = x_shift(split_halves(from_left, True), blk_size, x_size, 1)
    far_bottom = x_shift(split_halves(from_right, False), blk_size, x_size, -1)
    far = tuple(jnp.concatenate([a, b], axis=0) for a, b in zip(far_top, far_bottom))
    mine = (pieces, from_left, from_right, far)
    partner = core_swap(mine, bend_size)
    absolute = jnp.arange(2 * x_size, dtype=jnp.int32)
    abs_x, abs_c = absolute // 2, absolute % 2
    dx = (abs_x - x) % x_size
    dxi = jnp.array([0, 2, 3, 1], jnp.int32)[dx]
    order = (abs_c ^ core) * 4 + dxi
    return tuple(
        jnp.take(jnp.stack([mine[i][k] for i in range(4)] + [partner[i][k] for i in range(4)]),
                 order, axis=0)
        for k in range(len(pieces)))


def shards(
    queries,
    keys_values,
    surface,
    out_weight,
    up_weight,
    down_weight,
    norm_gain,
    block_lists,
    list_lengths,
):
    row_count, feature_width = queries.shape
    loop_size = lax.axis_size(("blk", "head"))
    blk_size = lax.axis_size("blk")
    bend_size = lax.axis_size("bend")
    x_size = 4
    own_index = lax.axis_index(("blk", "head"))
    x = lax.axis_index("blk") % x_size
    core = lax.axis_index("bend") % 2
    piece = x * 2 + core
    n_pieces = 2 * x_size

    out_rows = out_weight.shape[0] // n_pieces
    down_rows = down_weight.shape[0] // n_pieces
    up_cols = up_weight.shape[1] // n_pieces
    pieces = (
        lax.dynamic_slice_in_dim(out_weight, piece * out_rows, out_rows, axis=0),
        lax.dynamic_slice_in_dim(up_weight, piece * up_cols, up_cols, axis=1),
        lax.dynamic_slice_in_dim(down_weight, piece * down_rows, down_rows, axis=0),
    )
    sizes = [w.size for w in pieces]
    packed = jnp.concatenate([w.reshape(-1) for w in pieces])
    by_head = lax.all_gather(packed, "head", axis=0, tiled=False)
    (all_pieces,) = gather_over_x_and_core(
        (by_head,), blk_size, x_size, bend_size, x, core)
    n_heads = by_head.shape[0]
    d = feature_width
    o0, o1 = sizes[0], sizes[0] + sizes[1]
    out_full = jnp.transpose(
        all_pieces[:, :, :o0].reshape(n_pieces, n_heads, out_rows, d), (1, 0, 2, 3)).reshape(d, d)
    up_full = jnp.transpose(
        all_pieces[:, :, o0:o1].reshape(n_pieces, n_heads, -1, up_cols), (1, 2, 0, 3)
    ).reshape(d, n_pieces * up_cols)
    down_full = jnp.transpose(
        all_pieces[:, :, o1:].reshape(n_pieces, n_heads, down_rows, d), (1, 0, 2, 3)
    ).reshape(-1, d)

    blocks = [keys_values]
    ids = [own_index]
    left = right = keys_values
    for d in range(1, REACH + 1):
        left = ring_shift(left, ("blk", "head"), loop_size, 1)
        right = ring_shift(right, ("blk", "head"), loop_size, -1)
        blocks += [left, right]
        ids += [(own_index - d) % loop_size, (own_index + d) % loop_size]
    entry_live = jnp.arange(LIST, dtype=jnp.int32) < list_lengths[0]
    mask = jnp.stack(
        [jnp.any((block_lists[0] == b) & entry_live) for b in ids]).astype(jnp.int32)
    context = attend(mask, queries, blocks)

    hidden = surface.astype(jnp.float32) + jnp.dot(
        context, out_full, preferred_element_type=jnp.float32)
    mean_square = jnp.mean(hidden * hidden, axis=1, keepdims=True)
    normed = (hidden * lax.rsqrt(mean_square + 1e-05) * norm_gain[None, :]).astype(jnp.bfloat16)
    pre_gelu = jnp.dot(normed, up_full, preferred_element_type=jnp.float32)
    activated = jax.nn.gelu(pre_gelu, approximate=True).astype(jnp.bfloat16)
    mixed_out = hidden + jnp.dot(activated, down_full, preferred_element_type=jnp.float32)
    return mixed_out.astype(jnp.bfloat16)


def solution(mesh):
    return jax.shard_map(
        shards,
        mesh=mesh,
        in_specs=(
            P(("bend", "blk", "head"), None),
            P(None, ("bend", "blk", "head"), None),
            P(("bend", "blk", "head"), None),
            P("head", None),
            P("head", None),
            P("head", None),
            P(),
            P(("bend", "blk", "head"), None),
            P(("bend", "blk", "head")),
        ),
        out_specs=P(("bend", "blk", "head"), None),
        check_vma=False,
    )
```

profile of v0, /device:TPU:8, one launch (start us, length us, event | category | flops | bytes accessed | tf_op | source)
XLA Modules:
  0.0 205.6 jit_solution(12346609235928138228)
XLA Ops:
  6.5 1.1 copy-done
  7.7 0.9 constant_dynamic-slice_fusion
  8.6 0.8 constant_dynamic-slice_fusion.2
  9.5 0.7 pad_maximum_fusion.1
  10.2 2.0 collective-permute-start
  12.2 8.0 %collective-permute-start.1 = (bf16[2,256,768]{2,1,0:T(8,128)(2,1)}, bf16[2,256,768]{2,1,0:T(8,128)(2,1)S(1)}, u32[]{:S(2)}, u32[]{:S(2)}) collective-permute-start(bf16[2,256,768]{2,1,0:T(8,128)(2,1)} %refs_0_.1), channel_id=1, source_target_pairs={{0,252},{4,0},{8,4},{12,8},{16,12},{20,16},{24,20},{28,24},{32,28}... | collective-permute-start | bytes 2359304 | tf_op jit(solution)/shard_map/ppermute | solution.py:18
  20.8 22.5 %collective-permute-done.refs_1_ = bf16[2,256,768]{2,1,0:T(8,128)(2,1)S(1)} collective-permute-done((bf16[2,256,768]{2,1,0:T(8,128)(2,1)}, bf16[2,256,768]{2,1,0:T(8,128)(2,1)S(1)}, u32[]{:S(2)}, u32[]{:S(2)}) %collective-permute-start) | collective-permute-done | bytes 786464 | tf_op jit(solution)/shard_map/ppermute | solution.py:18
  43.3 3.7 %collective-permute-done.1.refs_2_ = bf16[2,256,768]{2,1,0:T(8,128)(2,1)S(1)} collective-permute-done((bf16[2,256,768]{2,1,0:T(8,128)(2,1)}, bf16[2,256,768]{2,1,0:T(8,128)(2,1)S(1)}, u32[]{:S(2)}, u32[]{:S(2)}) %collective-permute-start.1) | collective-permute-done | bytes 786464 | tf_op jit(solution)/shard_map/ppermute | solution.py:18
  47.0 8.1 %collective-permute-start.3 = (bf16[2,256,768]{2,1,0:T(8,128)(2,1)S(1)}, bf16[2,256,768]{2,1,0:T(8,128)(2,1)}, u32[]{:S(2)}, u32[]{:S(2)}) collective-permute-start(bf16[2,256,768]{2,1,0:T(8,128)(2,1)S(1)} %collective-permute-done.1.refs_2_), channel_id=1, source_target_pairs={{0,252},{4,0},{8,4},{12,8},{16,12},{20,16},{24,20},{28,24},{32,28}... | collective-permute-start | bytes 2359304 | tf_op jit(solution)/shard_map/ppermute | solution.py:18
  55.1 1.4 fusion.25
  56.5 4.4 %stack.58 = pred[7]{0:T(512)(128)(4,1)S(1)} concatenate(pred[1]{0:T(512)(128)(4,1)} %bitcast.2, pred[1]{0:T(512)(128)(4,1)} %bitcast.4, pred[1]{0:T(512)(128)(4,1)} %bitcast.6, pred[1]{0:T(512)(128)(4,1)} %bitcast.8, pred[1]{0:T(512)(128)(4,1)} %bitcast.10, pred[1]{0:T(512)(128)(4,1)} %bitcast.12, pred[1]{0:T(512)(128)(4,1)} %bitcast.14), dimensions={0} | concatenate | bytes 14 | tf_op jit(solution)/shard_map/stack | solution.py:200
  60.9 0.5 convert_element_type.16.mask_ref
  61.5 1.3 gather_fusion
  62.9 7.3 %collective-permute-done.2.refs_3_ = bf16[2,256,768]{2,1,0:T(8,128)(2,1)} collective-permute-done((bf16[2,256,768]{2,1,0:T(8,128)(2,1)S(1)}, bf16[2,256,768]{2,1,0:T(8,128)(2,1)}, u32[]{:S(2)}, u32[]{:S(2)}) %collective-permute-start.2) | collective-permute-done | bytes 786464 | tf_op jit(solution)/shard_map/ppermute | solution.py:18
  70.2 8.1 %collective-permute-start.5 = (bf16[2,256,768]{2,1,0:T(8,128)(2,1)}, bf16[2,256,768]{2,1,0:T(8,128)(2,1)}, u32[]{:S(2)}, u32[]{:S(2)}) collective-permute-start(bf16[2,256,768]{2,1,0:T(8,128)(2,1)} %collective-permute-done.3.refs_4_), channel_id=1, source_target_pairs={{0,252},{4,0},{8,4},{12,8},{16,12},{20,16},{24,20},{28,24},{32,28}... | collective-permute-start | bytes 2359304 | tf_op jit(solution)/shard_map/ppermute | solution.py:18
  78.3 3.1 %reshape.198 = bf16[8,82944]{1,0:T(8,128)(2,1)} reshape(bf16[663552]{0:T(1024)(128)(2,1)} %all-gather.3.cloned.1.call-done) | data formatting | bytes 2654208 | tf_op jit(solution)/shard_map/all_gather | solution.py:176
  81.4 3.2 %collective-permute-start.7 = (bf16[8,82944]{1,0:T(8,128)(2,1)}, bf16[8,82944]{1,0:T(8,128)(2,1)}, u32[]{:S(2)}, u32[]{:S(2)}) collective-permute-start(bf16[8,82944]{1,0:T(8,128)(2,1)} %reshape.198), channel_id=1, source_target_pairs={{0,96},{32,0},{64,32},{96,64},{128,224},{160,128},{192,160},{224,1... | collective-permute-start | bytes 3981320 | tf_op jit(solution)/shard_map/ppermute | solution.py:26
  84.6 0.6 stack.59
  85.2 1.2 constant_dynamic-update-slice_fusion
  86.4 8.1 %collective-permute-done.4.refs_5_ = bf16[2,256,768]{2,1,0:T(8,128)(2,1)} collective-permute-done((bf16[2,256,768]{2,1,0:T(8,128)(2,1)}, bf16[2,256,768]{2,1,0:T(8,128)(2,1)}, u32[]{:S(2)}, u32[]{:S(2)}) %collective-permute-start.4) | collective-permute-done | bytes 786464 | tf_op jit(solution)/shard_map/ppermute | solution.py:18
  94.5 23.4 %shard_map.100 = bf16[256,768]{1,0:T(8,128)(2,1)} custom-call(s32[7]{0:T(128)} %convert_element_type.16.mask_ref, bf16[256,768]{1,0:T(8,128)(2,1)} %q_ref.1, bf16[2,256,768]{2,1,0:T(8,128)(2,1)} %refs_0_.1, bf16[2,256,768]{2,1,0:T(8,128)(2,1)} %copy-done.4, bf16[2,256,768]{2,1,0:T(8,128)(2,1)} %copy-done.5, ...), custom_call_target="tpu_custom_call" | custom-call | flops 2415919104 | bytes 6291456 | tf_op jit(solution)/shard_map/pallas_call | solution.py:86
  117.9 3.3 %collective-permute-done.6 = bf16[8,82944]{1,0:T(8,128)(2,1)} collective-permute-done((bf16[8,82944]{1,0:T(8,128)(2,1)}, bf16[8,82944]{1,0:T(8,128)(2,1)}, u32[]{:S(2)}, u32[]{:S(2)}) %collective-permute-start.6) | collective-permute-done | bytes 1327136 | tf_op jit(solution)/shard_map/ppermute | solution.py:26
  121.2 1.5 slice.24
  122.8 1.7 slice.25
  124.5 3.3 %collective-permute-start.9 = (bf16[4,82944]{1,0:T(4,128)(2,1)S(1)}, bf16[4,82944]{1,0:T(4,128)(2,1)S(1)}, u32[]{:S(2)}, u32[]{:S(2)}) collective-permute-start(bf16[4,82944]{1,0:T(4,128)(2,1)S(1)} %slice.25), channel_id=1, source_target_pairs={{0,96},{32,0},{64,32},{96,64},{128,224},{160,128},{192,160},{224,1... | collective-permute-start | bytes 1990664 | tf_op jit(solution)/shard_map/ppermute | solution.py:26
  127.8 0.5 collective-permute-start.12
  128.3 2.5 %bitcast_dynamic-update-slice_fusion.6 = bf16[8,8,82944]{2,1,0:T(8,128)(2,1)} fusion(bf16[8,8,82944]{2,1,0:T(8,128)(2,1)} %constant_dynamic-update-slice_fusion, bf16[8,82944]{1,0:T(8,128)(2,1)} %collective-permute-done.6), kind=kLoop, calls=%fused_computation.24 | loop fusion | bytes 2654208
  130.8 2.5 %bitcast_dynamic-update-slice_fusion.5 = bf16[8,8,82944]{2,1,0:T(8,128)(2,1)} fusion(bf16[8,8,82944]{2,1,0:T(8,128)(2,1)} %bitcast_dynamic-update-slice_fusion.6, bf16[8,82944]{1,0:T(8,128)(2,1)} %collective-permute-done.7), kind=kLoop, calls=%fused_computation.23 | loop fusion | bytes 2654208
  133.3 7.6 %collective-permute-done.8 = bf16[4,82944]{1,0:T(4,128)(2,1)S(1)} collective-permute-done((bf16[4,82944]{1,0:T(4,128)(2,1)S(1)}, bf16[4,82944]{1,0:T(4,128)(2,1)S(1)}, u32[]{:S(2)}, u32[]{:S(2)}) %collective-permute-start.8) | collective-permute-done | bytes 663584 | tf_op jit(solution)/shard_map/ppermute | solution.py:26
  140.9 1.0 collective-permute-done.9
  141.9 0.6 pad_maximum_fusion
  142.5 0.3 collective-permute-start.13
  142.8 1.7 bitcast_dynamic-update-slice_fusion.4
  144.5 2.5 %bitcast_dynamic-update-slice_fusion.3 = bf16[8,8,82944]{2,1,0:T(8,128)(2,1)} fusion(bf16[8,8,82944]{2,1,0:T(8,128)(2,1)} %bitcast_dynamic-update-slice_fusion.4, bf16[8,82944]{1,0:T(8,128)(2,1)} %collective-permute-done.10), kind=kLoop, calls=%fused_computation.21 | loop fusion | bytes 2654208
  147.1 1.1 bitcast_dynamic-update-slice_fusion.2
  148.2 1.2 bitcast_dynamic-update-slice_fusion.1
  149.4 1.1 bitcast_dynamic-update-slice_fusion
  150.6 9.6 %gather_fusion.1 = bf16[8,8,82944]{2,1,0:T(8,128)(2,1)} fusion(bf16[8,8,82944]{2,1,0:T(8,128)(2,1)} %bitcast_dynamic-update-slice_fusion, s32[1024]{0:T(1024)S(1)} %pad_clamp_fusion), kind=kCustom, calls=%fused_computation.1 | custom fusion | bytes 21233696 | tf_op jit(solution)/shard_map/jit(_take)/gather | solution.py:139
  160.1 10.2 %broadcast_select_fusion = bf16[8,8,82944]{2,1,0:T(8,128)(2,1)} fusion(bf16[8,8,82944]{2,1,0:T(8,128)(2,1)} %gather_fusion.1, pred[8]{0:T(512)(128)(4,1)S(1)} %compare_and_fusion), kind=kLoop, calls=%fused_computation.2 | loop fusion | flops 5308416 | bytes 21233672 | tf_op jit(solution)/shard_map/jit(_take)/select_n | solution.py:139
  170.3 6.7 %fusion.46 = (bf16[8,8,36864]{2,1,0:T(8,128)(2,1)}, bf16[8,8,36864]{2,1,0:T(8,128)(2,1)S(1)}) fusion(bf16[8,8,82944]{2,1,0:T(8,128)(2,1)} %broadcast_select_fusion), kind=kLoop, calls=%fused_computation.83 | loop fusion | bytes 18874368 | tf_op jit(solution)/shard_map/slice | solution.py:185
  177.1 5.1 %copy.15 = bf16[8,8,96,384]{3,0,2,1:T(8,128)(2,1)S(1)} copy(bf16[8,8,96,384]{3,1,2,0:T(8,128)(2,1)} %bitcast.76) | data formatting | bytes 9437184 | tf_op jit(solution)/shard_map/reshape | solution.py:185
  182.2 3.3 %copy.17 = bf16[96,8,8,384]{3,1,2,0:T(8,128)(2,1)} copy(bf16[96,8,8,384]{3,2,1,0:T(8,128)(2,1)S(1)} %bitcast.74) | data formatting | bytes 9437184
  185.5 3.0 %copy.16 = bf16[8,8,48,768]{3,2,0,1:T(8,128)(2,1)} copy(bf16[8,8,48,768]{3,1,2,0:T(8,128)(2,1)S(1)} %bitcast.75) | data formatting | bytes 9437184 | tf_op jit(solution)/shard_map/reshape | solution.py:188
  188.6 0.3 copy.14
  188.9 0.3 reshape.177
  189.2 0.4 copy-done.3
  189.6 1.6 multiply_reduce_fusion
  191.2 7.6 %fusion.17 = bf16[256,768]{1,0:T(8,128)(2,1)} fusion(f32[256,768]{1,0:T(8,128)S(1)} %get-tuple-element.15, bf16[3072,768]{1,0:T(8,128)(2,1)} %bitcast.78, bf16[768,3072]{1,0:T(8,128)(2,1)} %bitcast.77, f32[768]{0:T(1024)S(1)} %copy-done.6, f32[256]{0:T(256)S(1)} %add_rsqrt_fusion), kind=kOutput, calls=%fused_computation.27 | convolution fusion | flops 2423980032 | bytes 10620928 | tf_op jit(solution)/shard_map/dot_general | solution.py:210
  (40 shorter events, 0.4 us)
Async XLA Ops:
  6.5 1.1 copy-start
  6.5 71.8 %all-gather.3.cloned.1.call-start = ((), (), s32[]{:S(2)}) async-start(), calls=%async_computation | async-start | bytes 1492992 | tf_op jit(solution)/shard_map/all_gather | solution.py:176
  10.2 33.1 %collective-permute-start = (bf16[2,256,768]{2,1,0:T(8,128)(2,1)}, bf16[2,256,768]{2,1,0:T(8,128)(2,1)S(1)}, u32[]{:S(2)}, u32[]{:S(2)}) collective-permute-start(bf16[2,256,768]{2,1,0:T(8,128)(2,1)} %refs_0_.1), channel_id=1, source_target_pairs={{0,4},{4,8},{8,12},{12,16},{16,20},{20,24},{24,28},{28,32},{32,36}... | collective-permute-start | bytes 2359304 | tf_op jit(solution)/shard_map/ppermute | solution.py:18
  12.2 34.8 %collective-permute-start.1 = (bf16[2,256,768]{2,1,0:T(8,128)(2,1)}, bf16[2,256,768]{2,1,0:T(8,128)(2,1)S(1)}, u32[]{:S(2)}, u32[]{:S(2)}) collective-permute-start(bf16[2,256,768]{2,1,0:T(8,128)(2,1)} %refs_0_.1), channel_id=1, source_target_pairs={{0,252},{4,0},{8,4},{12,8},{16,12},{20,16},{24,20},{28,24},{32,28}... | collective-permute-start | bytes 2359304 | tf_op jit(solution)/shard_map/ppermute | solution.py:18
  43.3 35.0 %copy-start.4 = (bf16[2,256,768]{2,1,0:T(8,128)(2,1)}, bf16[2,256,768]{2,1,0:T(8,128)(2,1)S(1)}, u32[]{:S(2)}) copy-start(bf16[2,256,768]{2,1,0:T(8,128)(2,1)S(1)} %collective-permute-done.refs_1_) | copy-start | bytes 2359300
  43.3 26.9 %collective-permute-start.2 = (bf16[2,256,768]{2,1,0:T(8,128)(2,1)S(1)}, bf16[2,256,768]{2,1,0:T(8,128)(2,1)}, u32[]{:S(2)}, u32[]{:S(2)}) collective-permute-start(bf16[2,256,768]{2,1,0:T(8,128)(2,1)S(1)} %collective-permute-done.refs_1_), channel_id=1, source_target_pairs={{0,4},{4,8},{8,12},{12,16},{16,20},{20,24},{24,28},{28,32},{32,36}... | collective-permute-start | bytes 2359304 | tf_op jit(solution)/shard_map/ppermute | solution.py:18
  47.0 31.3 %copy-start.5 = (bf16[2,256,768]{2,1,0:T(8,128)(2,1)}, bf16[2,256,768]{2,1,0:T(8,128)(2,1)S(1)}, u32[]{:S(2)}) copy-start(bf16[2,256,768]{2,1,0:T(8,128)(2,1)S(1)} %collective-permute-done.1.refs_2_) | copy-start | bytes 2359300
  47.0 23.2 %collective-permute-start.3 = (bf16[2,256,768]{2,1,0:T(8,128)(2,1)S(1)}, bf16[2,256,768]{2,1,0:T(8,128)(2,1)}, u32[]{:S(2)}, u32[]{:S(2)}) collective-permute-start(bf16[2,256,768]{2,1,0:T(8,128)(2,1)S(1)} %collective-permute-done.1.refs_2_), channel_id=1, source_target_pairs={{0,252},{4,0},{8,4},{12,8},{16,12},{20,16},{24,20},{28,24},{32,28}... | collective-permute-start | bytes 2359304 | tf_op jit(solution)/shard_map/ppermute | solution.py:18
  70.2 24.3 %collective-permute-start.4 = (bf16[2,256,768]{2,1,0:T(8,128)(2,1)}, bf16[2,256,768]{2,1,0:T(8,128)(2,1)}, u32[]{:S(2)}, u32[]{:S(2)}) collective-permute-start(bf16[2,256,768]{2,1,0:T(8,128)(2,1)} %collective-permute-done.2.refs_3_), channel_id=1, source_target_pairs={{0,4},{4,8},{8,12},{12,16},{16,20},{20,24},{24,28},{28,32},{32,36}... | collective-permute-start | bytes 2359304 | tf_op jit(solution)/shard_map/ppermute | solution.py:18
  70.2 24.3 %collective-permute-start.5 = (bf16[2,256,768]{2,1,0:T(8,128)(2,1)}, bf16[2,256,768]{2,1,0:T(8,128)(2,1)}, u32[]{:S(2)}, u32[]{:S(2)}) collective-permute-start(bf16[2,256,768]{2,1,0:T(8,128)(2,1)} %collective-permute-done.3.refs_4_), channel_id=1, source_target_pairs={{0,252},{4,0},{8,4},{12,8},{16,12},{20,16},{24,20},{28,24},{32,28}... | collective-permute-start | bytes 2359304 | tf_op jit(solution)/shard_map/ppermute | solution.py:18
  78.3 6.3 %copy-start.2 = (bf16[663552]{0:T(1024)(128)(2,1)S(1)}, bf16[663552]{0:T(1024)(128)(2,1)}, u32[]{:S(2)}) copy-start(bf16[663552]{0:T(1024)(128)(2,1)} %all-gather.3.cloned.1.call-done) | copy-start | bytes 3981316
  81.4 39.8 %collective-permute-start.6 = (bf16[8,82944]{1,0:T(8,128)(2,1)}, bf16[8,82944]{1,0:T(8,128)(2,1)}, u32[]{:S(2)}, u32[]{:S(2)}) collective-permute-start(bf16[8,82944]{1,0:T(8,128)(2,1)} %reshape.198), channel_id=1, source_target_pairs={{0,32},{32,64},{64,96},{96,0},{128,160},{160,192},{192,224},{224,1... | collective-permute-start | bytes 3981320 | tf_op jit(solution)/shard_map/ppermute | solution.py:26
  81.4 41.4 %collective-permute-start.7 = (bf16[8,82944]{1,0:T(8,128)(2,1)}, bf16[8,82944]{1,0:T(8,128)(2,1)}, u32[]{:S(2)}, u32[]{:S(2)}) collective-permute-start(bf16[8,82944]{1,0:T(8,128)(2,1)} %reshape.198), channel_id=1, source_target_pairs={{0,96},{32,0},{64,32},{96,64},{128,224},{160,128},{192,160},{224,1... | collective-permute-start | bytes 3981320 | tf_op jit(solution)/shard_map/ppermute | solution.py:26
  84.6 59.9 %collective-permute-start.10 = (bf16[8,82944]{1,0:T(8,128)(2,1)}, bf16[8,82944]{1,0:T(8,128)(2,1)}, u32[]{:S(2)}, u32[]{:S(2)}) collective-permute-start(bf16[8,82944]{1,0:T(8,128)(2,1)} %reshape.198), channel_id=1, source_target_pairs={{0,1},{1,0},{2,3},{3,2},{4,5},{5,4},{6,7},{7,6},{8,9},{9,8},{10,11... | collective-permute-start | bytes 3981320 | tf_op jit(solution)/shard_map/ppermute | solution.py:31
  122.7 18.1 %collective-permute-start.8 = (bf16[4,82944]{1,0:T(4,128)(2,1)S(1)}, bf16[4,82944]{1,0:T(4,128)(2,1)S(1)}, u32[]{:S(2)}, u32[]{:S(2)}) collective-permute-start(bf16[4,82944]{1,0:T(4,128)(2,1)S(1)} %slice.24), channel_id=1, source_target_pairs={{0,32},{32,64},{64,96},{96,0},{128,160},{160,192},{192,224},{224,1... | collective-permute-start | bytes 1990664 | tf_op jit(solution)/shard_map/ppermute | solution.py:26
  124.5 17.4 %collective-permute-start.9 = (bf16[4,82944]{1,0:T(4,128)(2,1)S(1)}, bf16[4,82944]{1,0:T(4,128)(2,1)S(1)}, u32[]{:S(2)}, u32[]{:S(2)}) collective-permute-start(bf16[4,82944]{1,0:T(4,128)(2,1)S(1)} %slice.25), channel_id=1, source_target_pairs={{0,96},{32,0},{64,32},{96,64},{128,224},{160,128},{192,160},{224,1... | collective-permute-start | bytes 1990664 | tf_op jit(solution)/shard_map/ppermute | solution.py:26
  127.8 19.3 %collective-permute-start.11 = (bf16[8,82944]{1,0:T(8,128)(2,1)}, bf16[8,82944]{1,0:T(8,128)(2,1)S(1)}, u32[]{:S(2)}, u32[]{:S(2)}) collective-permute-start(bf16[8,82944]{1,0:T(8,128)(2,1)} %collective-permute-done.6), channel_id=1, source_target_pairs={{0,1},{1,0},{2,3},{3,2},{4,5},{5,4},{6,7},{7,6},{8,9},{9,8},{10,11... | collective-permute-start | bytes 3981320 | tf_op jit(solution)/shard_map/ppermute | solution.py:31
  127.8 20.4 %collective-permute-start.12 = (bf16[8,82944]{1,0:T(8,128)(2,1)}, bf16[8,82944]{1,0:T(8,128)(2,1)S(1)}, u32[]{:S(2)}, u32[]{:S(2)}) collective-permute-start(bf16[8,82944]{1,0:T(8,128)(2,1)} %collective-permute-done.7), channel_id=1, source_target_pairs={{0,1},{1,0},{2,3},{3,2},{4,5},{5,4},{6,7},{7,6},{8,9},{9,8},{10,11... | collective-permute-start | bytes 3981320 | tf_op jit(solution)/shard_map/ppermute | solution.py:31
  142.5 6.9 %collective-permute-start.13 = (bf16[8,82944]{1,0:T(8,128)(2,1)S(1)}, bf16[8,82944]{1,0:T(8,128)(2,1)S(1)}, u32[]{:S(2)}, u32[]{:S(2)}) collective-permute-start(bf16[8,82944]{1,0:T(8,128)(2,1)S(1)} %pad_maximum_fusion), channel_id=1, source_target_pairs={{0,1},{1,0},{2,3},{3,2},{4,5},{5,4},{6,7},{7,6},{8,9},{9,8},{10,11... | collective-permute-start | bytes 3981320 | tf_op jit(solution)/shard_map/ppermute | solution.py:31
  185.5 3.1 %slice-start = ((bf16[8,8,82944]{2,1,0:T(8,128)(2,1)}), bf16[8,8,9216]{2,1,0:T(8,128)(2,1)S(1)}, s32[]{:S(2)}) async-start(bf16[8,8,82944]{2,1,0:T(8,128)(2,1)} %broadcast_select_fusion), calls=%async_computation.1 | async-start | bytes 2359296 | tf_op jit(solution)/shard_map/slice | solution.py:183
  188.6 1.0 copy-start.3
  188.9 2.3 %copy-start.6 = (f32[768]{0:T(1024)S(1)}, f32[768]{0:T(1024)}, u32[]{:S(2)}) copy-start(f32[768]{0:T(1024)} %param.16) | copy-start | bytes 9220
  191.2 7.6 %copy-start.1 = (bf16[96,3072]{1,0:T(8,128)(2,1)S(1)}, bf16[96,3072]{1,0:T(8,128)(2,1)}, u32[]{:S(2)}) copy-start(bf16[96,3072]{1,0:T(8,128)(2,1)} %param.14) | copy-start | bytes 1769476
Sparse Core Ops, SparseCore 0:
  10.3 45.4 all-gather.2
where the time goes:
time: 208 us; the launch traced here: 206 us
  local copies, waits for them, and re-layouts  56.4 us (27%)
  waiting for transfers between devices  53.6 us (26%)
  starting transfers between devices  33.6 us (16%)
  Pallas kernels  23.4 us (11%)
  other arithmetic  15.3 us (7%)
  between operations  14.2 us (7%)
  matrix products  9.12 us (4%)
    ppermute x6, waiting for transfers between devices, ring_shift(): return lax.ppermute(block, axis, route)  41.7 us
    ppermute x6, starting transfers between devices, ring_shift(): return lax.ppermute(block, axis, route)  26.2 us
    pallas_call x1, Pallas kernels, attend(): pl.pallas_call(functools.partial(attention_kernel, n_blocks), grid_spec=g...  23.4 us
    unnamed x21, local copies, waits for them, and re-layouts  15.8 us
    ppermute x4, waiting for transfers between devices, x_shift(): return lax.ppermute(block, 'blk', route)  11.9 us
    select_n x2, other arithmetic, gather_over_x_and_core(): jnp.take(jnp.stack([mine[i][k] for i in range(4)] + [partner[i][k] for i...  10.2 us
    gather x1, local copies, waits for them, and re-layouts, gather_over_x_and_core(): jnp.take(jnp.stack([mine[i][k] for i in range(4)] + [partner[i][k] for i...  9.56 us
    dot_general x1, matrix products, shards(): jnp.dot(activated, down_full, preferred_element_type=jnp.float32)  7.57 us
  transfers between devices with their start and end apart: 15, of which 7 were waited for; matrix products, arithmetic and copies ran while one was open for 14% of the time, Pallas kernels for 11%

commit v1 on v0

--- a/solution.py
+++ b/solution.py
@@ -11,6 +11,7 @@
 HD = 64
 LIST = 4
 REACH = 3
+MESH = pl.DeviceIdType.MESH
 
 
 def ring_shift(block, axis, size, distance):
@@ -95,50 +96,115 @@
     )(mask, q, *blocks)
 
 
-def order_of(offsets, me, n):
-    held = (me + jnp.array(offsets, jnp.int32)) % n
-    return jnp.argmax(held[None, :] == jnp.arange(n, dtype=jnp.int32)[:, None], axis=1)
-
-
-def split_halves(tree, take_first):
-    return tuple(w[: w.shape[0] // 2] if take_first else w[w.shape[0] // 2:] for w in tree)
-
-
-def gather_over_head(pieces, n):
-    me = lax.axis_index("head")
-    rel, offsets = [pieces], [0]
-    left = right = pieces
-    for k in range(1, n // 2):
-        left = ring_shift(left, "head", n, 1)
-        right = ring_shift(right, "head", n, -1)
-        rel += [left, right]
-        offsets += [-k, k]
-    far_top = ring_shift(split_halves(left, True), "head", n, 1)
-    far_bottom = ring_shift(split_halves(right, False), "head", n, -1)
-    rel.append(tuple(jnp.concatenate([a, b], axis=0) for a, b in zip(far_top, far_bottom)))
-    offsets.append(n // 2)
-    order = order_of(offsets, me, n)
-    return tuple(jnp.take(jnp.stack([r[k] for r in rel]), order, axis=0)
-                 for k in range(len(pieces)))
-
-
-def gather_over_x_and_core(pieces, blk_size, x_size, bend_size, x, core):
-    from_left = x_shift(pieces, blk_size, x_size, 1)
-    from_right = x_shift(pieces, blk_size, x_size, -1)
-    far_top = x_shift(split_halves(from_left, True), blk_size, x_size, 1)
-    far_bottom = x_shift(split_halves(from_right, False), blk_size, x_size, -1)
-    far = tuple(jnp.concatenate([a, b], axis=0) for a, b in zip(far_top, far_bottom))
-    mine = (pieces, from_left, from_right, far)
-    partner = core_swap(mine, bend_size)
-    absolute = jnp.arange(2 * x_size, dtype=jnp.int32)
-    abs_x, abs_c = absolute // 2, absolute % 2
-    dx = (abs_x - x) % x_size
-    dxi = jnp.array([0, 2, 3, 1], jnp.int32)[dx]
-    order = (abs_c ^ core) * 4 + dxi
-    return tuple(
-        jnp.take(jnp.stack([mine[i][k] for i in range(4)] + [partner[i][k] for i in range(4)]),
-                 order, axis=0)
-        for k in range(len(pieces)))
+def spread_kernel(x_size, up_z, down_z, out_z, up_full, down_full, out_full,
+                  send_sems, recv_sems, local_sems):
+    blk = lax.axis_index("blk")
+    head = lax.axis_index("head")
+    bend = lax.axis_index("bend")
+    hi, x = blk // x_size, blk % x_size
+    c = bend % 2
+    left = (hi * x_size + (x + x_size - 1) % x_size, head, bend)
+    right = (hi * x_size + (x + 1) % x_size, head, bend)
+    partner = (blk, head, bend + 1 - 2 * c)
+    p_own = x * 2 + c
+    p_left = ((x + x_size - 1) % x_size) * 2 + c
+    p_right = ((x + 1) % x_size) * 2 + c
+    p_far = ((x + 2) % x_size) * 2 + c
+    width = up_z.shape[1]
+    rows = up_z.shape[0]
+    heads = down_z.shape[0]
+
+    barrier = pltpu.get_barrier_semaphore()
+    for dev in (left, right, partner):
+        pl.semaphore_signal(barrier, inc=1, device_id=dev, device_id_type=MESH)
+    pl.semaphore_wait(barrier, 3)
+
+    def up_at(p, part=None):
+        cols = pl.ds(pl.multiple_of(p * width, 128), width)
+        if part is None:
+            return up_full.at[:, cols]
+        return up_full.at[pl.ds(part * (rows // 2), rows // 2), cols]
+
+    def down_at(p, part=None):
+        if part is None:
+            return down_full.at[:, p]
+        return down_full.at[pl.ds(part * (heads // 2), heads // 2), p]
+
+    def send(src, dst, k, dev):
+        copy = pltpu.make_async_remote_copy(
+            src_ref=src, dst_ref=dst, send_sem=send_sems.at[k], recv_sem=recv_sems.at[k],
+            device_id=dev, device_id_type=MESH)
+        copy.start()
+        return copy
+
+    local = [
+        pltpu.make_async_copy(up_z, up_at(p_own), local_sems.at[0]),
+        pltpu.make_async_copy(down_z, down_at(p_own), local_sems.at[1]),
+        pltpu.make_async_copy(out_z, out_full.at[:, c], local_sems.at[2]),
+    ]
+    for copy in local:
+        copy.start()
+    a_up_r = send(up_z, up_at(p_own), 0, right)
+    a_up_l = send(up_z, up_at(p_own), 1, left)
+    a_dn_r = send(down_z, down_at(p_own), 2, right)
+    a_dn_l = send(down_z, down_at(p_own), 3, left)
+    sent = [a_up_r, a_up_l, a_dn_r, a_dn_l]
+    sent += [
+        send(out_z, out_full.at[:, c], 4, partner),
+        send(up_z, up_at(p_own), 5, partner),
+        send(down_z, down_at(p_own), 6, partner),
+    ]
+    a_up_r.wait_recv()
+    a_dn_r.wait_recv()
+    b_up_r = send(up_at(p_left, 0), up_at(p_left, 0), 7, right)
+    b_dn_r = send(down_at(p_left, 0), down_at(p_left, 0), 8, right)
+    sent += [b_up_r, b_dn_r]
+    sent += [send(up_at(p_left), up_at(p_left), 9, partner),
+             send(down_at(p_left), down_at(p_left), 10, partner)]
+    a_up_l.wait_recv()
+    a_dn_l.wait_recv()
+    b_up_l = send(up_at(p_right, 1), up_at(p_right, 1), 11, left)
+    b_dn_l = send(down_at(p_right, 1), down_at(p_right, 1), 12, left)
+    sent += [b_up_l, b_dn_l]
+    sent += [send(up_at(p_right), up_at(p_right), 13, partner),
+             send(down_at(p_right), down_at(p_right), 14, partner)]
+    b_up_r.wait_recv()
+    b_dn_r.wait_recv()
+    sent += [send(up_at(p_far, 0), up_at(p_far, 0), 15, partner),
+             send(down_at(p_far, 0), down_at(p_far, 0), 16, partner)]
+    b_up_l.wait_recv()
+    b_dn_l.wait_recv()
+    sent += [send(up_at(p_far, 1), up_at(p_far, 1), 17, partner),
+             send(down_at(p_far, 1), down_at(p_far, 1), 18, partner)]
+    for k in (4, 5, 6, 9, 10, 13, 14, 15, 16, 17, 18):
+        sent[k].wait_recv()
+    for copy in sent:
+        copy.wait_send()
+    for copy in local:
+        copy.wait()
+
+
+def spread_weights(up_z, down_z, out_z, x_size):
+    rows, width = up_z.shape
+    heads, down_rows, d = down_z.shape
+    n_pieces = 2 * x_size
+    any_spec = pl.BlockSpec(memory_space=pl.ANY)
+    return pl.pallas_call(
+        functools.partial(spread_kernel, x_size),
+        out_shape=(
+            jax.ShapeDtypeStruct((rows, n_pieces * width), up_z.dtype),
+            jax.ShapeDtypeStruct((heads, n_pieces, down_rows, d), down_z.dtype),
+            jax.ShapeDtypeStruct((heads, 2) + out_z.shape[1:], out_z.dtype),
+        ),
+        in_specs=[any_spec] * 3,
+        out_specs=(any_spec, any_spec, any_spec),
+        scratch_shapes=[
+            pltpu.SemaphoreType.DMA((19,)),
+            pltpu.SemaphoreType.DMA((19,)),
+            pltpu.SemaphoreType.DMA((3,)),
+        ],
+        compiler_params=pltpu.CompilerParams(collective_id=1, has_side_effects=True),
+    )(up_z, down_z, out_z)
 
 
 def shards(
@@ -163,30 +229,26 @@
     piece = x * 2 + core
     n_pieces = 2 * x_size
 
-    out_rows = out_weight.shape[0] // n_pieces
+    out_rows = out_weight.shape[0] // 2
     down_rows = down_weight.shape[0] // n_pieces
     up_cols = up_weight.shape[1] // n_pieces
     pieces = (
-        lax.dynamic_slice_in_dim(out_weight, piece * out_rows, out_rows, axis=0),
+        lax.dynamic_slice_in_dim(out_weight, core * out_rows, out_rows, axis=0),
         lax.dynamic_slice_in_dim(up_weight, piece * up_cols, up_cols, axis=1),
         lax.dynamic_slice_in_dim(down_weight, piece * down_rows, down_rows, axis=0),
     )
     sizes = [w.size for w in pieces]
     packed = jnp.concatenate([w.reshape(-1) for w in pieces])
     by_head = lax.all_gather(packed, "head", axis=0, tiled=False)
-    (all_pieces,) = gather_over_x_and_core(
-        (by_head,), blk_size, x_size, bend_size, x, core)
     n_heads = by_head.shape[0]
     d = feature_width
     o0, o1 = sizes[0], sizes[0] + sizes[1]
-    out_full = jnp.transpose(
-        all_pieces[:, :, :o0].reshape(n_pieces, n_heads, out_rows, d), (1, 0, 2, 3)).reshape(d, d)
-    up_full = jnp.transpose(
-        all_pieces[:, :, o0:o1].reshape(n_pieces, n_heads, -1, up_cols), (1, 2, 0, 3)
-    ).reshape(d, n_pieces * up_cols)
-    down_full = jnp.transpose(
-        all_pieces[:, :, o1:].reshape(n_pieces, n_heads, down_rows, d), (1, 0, 2, 3)
-    ).reshape(-1, d)
+    out_z = by_head[:, :o0].reshape(n_heads, out_rows, d)
+    up_z = by_head[:, o0:o1].reshape(-1, up_cols)
+    down_z = by_head[:, o1:].reshape(n_heads, down_rows, d)
+    up_full, down_full, out_full = spread_weights(up_z, down_z, out_z, x_size)
+    out_full = out_full.reshape(d, d)
+    down_full = down_full.reshape(-1, d)
 
     blocks = [keys_values]
     ids = [own_index]

time: 208 us -> 201 us (0.966)
  Pallas kernels: 23.4 us -> 78.6 us
  local copies, waits for them, and re-layouts: 56.4 us -> 13.3 us
  other arithmetic: 15.3 us -> 2.76 us
  starting transfers between devices: 33.6 us -> 25.8 us
    pallas_call x0 -> x1, Pallas kernels: none -> 55.1 us  [spread_weights(): pl.pallas_call(functools.partial(spread_kernel, x_size), out_shape=(jax.S...]
    unnamed x21 -> x14, local copies, waits for them, and re-layouts: 15.8 us -> 0.08 us
    ppermute x6, waiting for transfers between devices: 41.7 us -> 53.9 us  [ring_shift(): return lax.ppermute(block, axis, route)]
    ppermute x8 -> x0, waiting for transfers between devices: 11.9 us -> none  [the longest x4 11.9 us: x_shift(): return lax.ppermute(block, 'blk', route)]
    gather x2 -> x0, local copies, waits for them, and re-layouts: 10.9 us -> none  [the longest x1 9.56 us: gather_over_x_and_core(): jnp.take(jnp.stack([mine[i][k] for i in range(4)] + [partner[i][k] for i...]
    select_n x3 -> x0, other arithmetic: 10.2 us -> none  [the longest x2 10.2 us: gather_over_x_and_core(): jnp.take(jnp.stack([mine[i][k] for i in range(4)] + [partner[i][k] for i...]
    slice x5 -> x1, local copies, waits for them, and re-layouts: 9.91 us -> 0.92 us  [shards(): out_z = by_head[:, :o0].reshape(n_heads, out_rows, d)]
    ppermute x8 -> x0, starting transfers between devices: 7.44 us -> none  [the longest x4 6.61 us: x_shift(): return lax.ppermute(block, 'blk', route)]
  transfers between devices with their start and end apart: 15 -> 7, of which waited for: 7 -> 4; matrix products, arithmetic and copies ran while one was open for 14% -> 3% of each run, Pallas kernels for 11% -> 12%
where the time goes in v1:
time: 201 us; the launch traced here: 198 us
  Pallas kernels  78.6 us (39%)
  waiting for transfers between devices  53.9 us (27%)
  starting transfers between devices  25.8 us (13%)
  between operations  14.2 us (7%)
  local copies, waits for them, and re-layouts  13.3 us (7%)
  matrix products  9.36 us (5%)
  other arithmetic  2.76 us (1%)
    pallas_call x1, Pallas kernels, spread_weights(): pl.pallas_call(functools.partial(spread_kernel, x_size), out_shape=(jax.S...  55.1 us
    ppermute x6, waiting for transfers between devices, ring_shift(): return lax.ppermute(block, axis, route)  53.9 us
    ppermute x6, starting transfers between devices, ring_shift(): return lax.ppermute(block, axis, route)  25.8 us
    pallas_call x1, Pallas kernels, attend(): pl.pallas_call(functools.partial(attention_kernel, n_blocks), grid_spec=g...  23.5 us
    dot_general x1, matrix products, shards(): jnp.dot(activated, down_full, preferred_element_type=jnp.float32)  7.53 us
    another operation x1, local copies, waits for them, and re-layouts, shards(): jnp.stack([jnp.any((block_lists[0] == b) & entry_live) for b in ids])  4.6 us
  transfers between devices with their start and end apart: 7, of which 4 were waited for; matrix products, arithmetic and copies ran while one was open for 3% of the time, Pallas kernels for 12%

profile of v1, /device:TPU:8, one launch (start us, length us, event | category | flops | bytes accessed | tf_op | source)
XLA Modules:
  0.0 197.8 jit_solution(266486417078720432)
XLA Ops:
  6.5 0.0 copy-start
  6.5 0.0 all-gather.3.cloned.1.call-start
  6.5 1.0 constant_dynamic-slice_fusion.2
  7.5 0.1 reshape.47
  7.6 0.1 copy-done
  7.7 0.9 constant_dynamic-slice_fusion
  8.6 0.1 reshape.49
  8.7 0.7 pad_maximum_fusion
  9.4 0.0 all-gather.3.cloned.1.call-update
  9.4 2.0 %collective-permute-start = (bf16[2,256,768]{2,1,0:T(8,128)(2,1)}, bf16[2,256,768]{2,1,0:T(8,128)(2,1)S(1)}, u32[]{:S(2)}, u32[]{:S(2)}) collective-permute-start(bf16[2,256,768]{2,1,0:T(8,128)(2,1)} %refs_0_.1), channel_id=1, source_target_pairs={{0,4},{4,8},{8,12},{12,16},{16,20},{20,24},{24,28},{28,32},{32,36}... | collective-permute-start | bytes 2359304 | tf_op jit(solution)/shard_map/ppermute | solution.py:19
  11.4 8.0 %collective-permute-start.1 = (bf16[2,256,768]{2,1,0:T(8,128)(2,1)}, bf16[2,256,768]{2,1,0:T(8,128)(2,1)S(1)}, u32[]{:S(2)}, u32[]{:S(2)}) collective-permute-start(bf16[2,256,768]{2,1,0:T(8,128)(2,1)} %refs_0_.1), channel_id=1, source_target_pairs={{0,252},{4,0},{8,4},{12,8},{16,12},{20,16},{24,20},{28,24},{32,28}... | collective-permute-start | bytes 2359304 | tf_op jit(solution)/shard_map/ppermute | solution.py:19
  19.3 24.3 %collective-permute-done.refs_1_ = bf16[2,256,768]{2,1,0:T(8,128)(2,1)S(1)} collective-permute-done((bf16[2,256,768]{2,1,0:T(8,128)(2,1)}, bf16[2,256,768]{2,1,0:T(8,128)(2,1)S(1)}, u32[]{:S(2)}, u32[]{:S(2)}) %collective-permute-start) | collective-permute-done | bytes 786464 | tf_op jit(solution)/shard_map/ppermute | solution.py:19
  43.6 0.0 copy-start.3
  43.6 0.0 collective-permute-start.2
  43.6 5.3 %collective-permute-done.1.refs_2_ = bf16[2,256,768]{2,1,0:T(8,128)(2,1)S(1)} collective-permute-done((bf16[2,256,768]{2,1,0:T(8,128)(2,1)}, bf16[2,256,768]{2,1,0:T(8,128)(2,1)S(1)}, u32[]{:S(2)}, u32[]{:S(2)}) %collective-permute-start.1) | collective-permute-done | bytes 786464 | tf_op jit(solution)/shard_map/ppermute | solution.py:19
  48.9 0.0 copy-start.4
  48.9 8.1 %collective-permute-start.3 = (bf16[2,256,768]{2,1,0:T(8,128)(2,1)S(1)}, bf16[2,256,768]{2,1,0:T(8,128)(2,1)}, u32[]{:S(2)}, u32[]{:S(2)}) collective-permute-start(bf16[2,256,768]{2,1,0:T(8,128)(2,1)S(1)} %collective-permute-done.1.refs_2_), channel_id=1, source_target_pairs={{0,252},{4,0},{8,4},{12,8},{16,12},{20,16},{24,20},{28,24},{32,28}... | collective-permute-start | bytes 2359304 | tf_op jit(solution)/shard_map/ppermute | solution.py:19
  57.0 15.6 %collective-permute-done.2.refs_3_ = bf16[2,256,768]{2,1,0:T(8,128)(2,1)S(1)} collective-permute-done((bf16[2,256,768]{2,1,0:T(8,128)(2,1)S(1)}, bf16[2,256,768]{2,1,0:T(8,128)(2,1)S(1)}, u32[]{:S(2)}, u32[]{:S(2)}) %collective-permute-start.2) | collective-permute-done | bytes 786464 | tf_op jit(solution)/shard_map/ppermute | solution.py:19
  72.6 0.0 copy-start.5
  72.6 0.0 collective-permute-start.4
  72.7 0.0 collective-permute-done.3.refs_4_
  72.7 7.7 %collective-permute-start.5 = (bf16[2,256,768]{2,1,0:T(8,128)(2,1)}, bf16[2,256,768]{2,1,0:T(8,128)(2,1)}, u32[]{:S(2)}, u32[]{:S(2)}) collective-permute-start(bf16[2,256,768]{2,1,0:T(8,128)(2,1)} %collective-permute-done.3.refs_4_), channel_id=1, source_target_pairs={{0,252},{4,0},{8,4},{12,8},{16,12},{20,16},{24,20},{28,24},{32,28}... | collective-permute-start | bytes 2359304 | tf_op jit(solution)/shard_map/ppermute | solution.py:19
  81.1 1.5 fusion.25
  82.6 4.6 %stack.31 = pred[7]{0:T(512)(128)(4,1)S(1)} concatenate(pred[1]{0:T(512)(128)(4,1)} %bitcast.2, pred[1]{0:T(512)(128)(4,1)} %bitcast.4, pred[1]{0:T(512)(128)(4,1)} %bitcast.6, pred[1]{0:T(512)(128)(4,1)} %bitcast.8, pred[1]{0:T(512)(128)(4,1)} %bitcast.10, pred[1]{0:T(512)(128)(4,1)} %bitcast.12, pred[1]{0:T(512)(128)(4,1)} %bitcast.14), dimensions={0} | concatenate | bytes 14 | tf_op jit(solution)/shard_map/stack | solution.py:262
  87.2 0.6 convert_element_type.16.mask_ref
  87.7 8.7 %collective-permute-done.4.refs_5_ = bf16[2,256,768]{2,1,0:T(8,128)(2,1)} collective-permute-done((bf16[2,256,768]{2,1,0:T(8,128)(2,1)S(1)}, bf16[2,256,768]{2,1,0:T(8,128)(2,1)}, u32[]{:S(2)}, u32[]{:S(2)}) %collective-permute-start.4) | collective-permute-done | bytes 786464 | tf_op jit(solution)/shard_map/ppermute | solution.py:19
  96.4 0.0 collective-permute-done.5.refs_6_
  96.4 0.0 copy-done.3
  96.4 0.0 copy-done.4
  96.4 0.0 copy-done.5
  96.4 23.5 %shard_map.91 = bf16[256,768]{1,0:T(8,128)(2,1)} custom-call(s32[7]{0:T(128)} %convert_element_type.16.mask_ref, bf16[256,768]{1,0:T(8,128)(2,1)} %q_ref.1, bf16[2,256,768]{2,1,0:T(8,128)(2,1)} %refs_0_.1, bf16[2,256,768]{2,1,0:T(8,128)(2,1)} %copy-done.3, bf16[2,256,768]{2,1,0:T(8,128)(2,1)} %copy-done.4, bf16[2,256,768]{2,1,0:T(8,128)(2,1)} %copy-done.5, ...), custom_call_target="tpu_custom_call" | custom-call | flops 2415919104 | bytes 6291456 | tf_op jit(solution)/shard_map/pallas_call | solution.py:87
  119.9 0.0 all-gather.3.cloned.1.call-done
  119.9 2.2 %reshape.55 = bf16[8,110592]{1,0:T(8,128)(2,1)S(1)} reshape(bf16[884736]{0:T(1024)(128)(2,1)} %all-gather.3.cloned.1.call-done) | data formatting | bytes 3538944 | tf_op jit(solution)/shard_map/all_gather | solution.py:242
  122.1 0.9 fusion.36
  123.1 0.0 copy-start.1
  123.1 0.0 copy-start.2
  123.1 1.1 reshape.50.up_z
  124.2 0.0 copy-start.6
  124.2 2.3 %copy_bitcast_fusion = (bf16[8,48,768]{2,1,0:T(8,128)(2,1)}, bf16[8,48,768]{2,1,0:T(8,128)(2,1)}) fusion(bf16[1,8,48,768]{3,1,2,0:T(8,128)(2,1)S(1)} %bitcast.49, bf16[1,8,48,768]{3,1,2,0:T(8,128)(2,1)} %bitcast.50), kind=kLoop, calls=%fused_computation.19 | loop fusion | bytes 2359296 | tf_op jit(solution)/shard_map/reshape | solution.py:246
  126.5 55.1 %shard_map.92 = (bf16[768,3072]{1,0:T(8,128)(2,1)}, bf16[8,8,48,768]{3,2,1,0:T(8,128)(2,1)}, bf16[8,2,48,768]{3,2,1,0:T(8,128)(2,1)}) custom-call(bf16[768,384]{1,0:T(8,128)(2,1)} %reshape.50.up_z, bf16[8,48,768]{2,1,0:T(8,128)(2,1)} %get-tuple-element.24.down_z, bf16[8,48,768]{2,1,0:T(8,128)(2,1)} %get-tuple-element.23.out_z), custom_call_target="tpu_custom_call" | custom-call | tf_op jit(solution)/shard_map/pallas_call | solution.py:192
  181.5 0.0 copy-done.1
  181.5 0.0 copy-done.2
  181.6 1.8 multiply_reduce_fusion
  183.4 0.0 copy-done.6
  183.4 7.5 %fusion.17 = bf16[256,768]{1,0:T(8,128)(2,1)} fusion(f32[256,768]{1,0:T(8,128)S(1)} %get-tuple-element.22, bf16[3072,768]{1,0:T(8,128)(2,1)} %bitcast.52, bf16[768,3072]{1,0:T(8,128)(2,1)} %get-tuple-element.9, f32[768]{0:T(1024)S(1)} %copy-done.6, f32[256]{0:T(256)S(1)} %add_rsqrt_fusion), kind=kOutput, calls=%fused_computation.16 | convolution fusion | flops 2423980032 | bytes 10620928 | tf_op jit(solution)/shard_map/dot_general | solution.py:272
  (3 shorter events, 0.1 us)
Async XLA Ops:
  6.5 1.1 copy-start
  6.5 113.4 %all-gather.3.cloned.1.call-start = ((), (), s32[]{:S(2)}) async-start(), calls=%async_computation | async-start | bytes 1990656 | tf_op jit(solution)/shard_map/all_gather | solution.py:242
  9.4 34.2 %collective-permute-start = (bf16[2,256,768]{2,1,0:T(8,128)(2,1)}, bf16[2,256,768]{2,1,0:T(8,128)(2,1)S(1)}, u32[]{:S(2)}, u32[]{:S(2)}) collective-permute-start(bf16[2,256,768]{2,1,0:T(8,128)(2,1)} %refs_0_.1), channel_id=1, source_target_pairs={{0,4},{4,8},{8,12},{12,16},{16,20},{20,24},{24,28},{28,32},{32,36}... | collective-permute-start | bytes 2359304 | tf_op jit(solution)/shard_map/ppermute | solution.py:19
  11.4 37.6 %collective-permute-start.1 = (bf16[2,256,768]{2,1,0:T(8,128)(2,1)}, bf16[2,256,768]{2,1,0:T(8,128)(2,1)S(1)}, u32[]{:S(2)}, u32[]{:S(2)}) collective-permute-start(bf16[2,256,768]{2,1,0:T(8,128)(2,1)} %refs_0_.1), channel_id=1, source_target_pairs={{0,252},{4,0},{8,4},{12,8},{16,12},{20,16},{24,20},{28,24},{32,28}... | collective-permute-start | bytes 2359304 | tf_op jit(solution)/shard_map/ppermute | solution.py:19
  43.6 52.8 %copy-start.3 = (bf16[2,256,768]{2,1,0:T(8,128)(2,1)}, bf16[2,256,768]{2,1,0:T(8,128)(2,1)S(1)}, u32[]{:S(2)}) copy-start(bf16[2,256,768]{2,1,0:T(8,128)(2,1)S(1)} %collective-permute-done.refs_1_) | copy-start | bytes 2359300
  43.6 29.0 %collective-permute-start.2 = (bf16[2,256,768]{2,1,0:T(8,128)(2,1)S(1)}, bf16[2,256,768]{2,1,0:T(8,128)(2,1)S(1)}, u32[]{:S(2)}, u32[]{:S(2)}) collective-permute-start(bf16[2,256,768]{2,1,0:T(8,128)(2,1)S(1)} %collective-permute-done.refs_1_), channel_id=1, source_target_pairs={{0,4},{4,8},{8,12},{12,16},{16,20},{20,24},{24,28},{28,32},{32,36}... | collective-permute-start | bytes 2359304 | tf_op jit(solution)/shard_map/ppermute | solution.py:19
  48.9 47.5 %copy-start.4 = (bf16[2,256,768]{2,1,0:T(8,128)(2,1)}, bf16[2,256,768]{2,1,0:T(8,128)(2,1)S(1)}, u32[]{:S(2)}) copy-start(bf16[2,256,768]{2,1,0:T(8,128)(2,1)S(1)} %collective-permute-done.1.refs_2_) | copy-start | bytes 2359300
  48.9 23.7 %collective-permute-start.3 = (bf16[2,256,768]{2,1,0:T(8,128)(2,1)S(1)}, bf16[2,256,768]{2,1,0:T(8,128)(2,1)}, u32[]{:S(2)}, u32[]{:S(2)}) collective-permute-start(bf16[2,256,768]{2,1,0:T(8,128)(2,1)S(1)} %collective-permute-done.1.refs_2_), channel_id=1, source_target_pairs={{0,252},{4,0},{8,4},{12,8},{16,12},{20,16},{24,20},{28,24},{32,28}... | collective-permute-start | bytes 2359304 | tf_op jit(solution)/shard_map/ppermute | solution.py:19
  72.6 23.8 %copy-start.5 = (bf16[2,256,768]{2,1,0:T(8,128)(2,1)}, bf16[2,256,768]{2,1,0:T(8,128)(2,1)S(1)}, u32[]{:S(2)}) copy-start(bf16[2,256,768]{2,1,0:T(8,128)(2,1)S(1)} %collective-permute-done.2.refs_3_) | copy-start | bytes 2359300
  72.6 23.8 %collective-permute-start.4 = (bf16[2,256,768]{2,1,0:T(8,128)(2,1)S(1)}, bf16[2,256,768]{2,1,0:T(8,128)(2,1)}, u32[]{:S(2)}, u32[]{:S(2)}) collective-permute-start(bf16[2,256,768]{2,1,0:T(8,128)(2,1)S(1)} %collective-permute-done.2.refs_3_), channel_id=1, source_target_pairs={{0,4},{4,8},{8,12},{12,16},{16,20},{20,24},{24,28},{28,32},{32,36}... | collective-permute-start | bytes 2359304 | tf_op jit(solution)/shard_map/ppermute | solution.py:19
  72.7 23.7 %collective-permute-start.5 = (bf16[2,256,768]{2,1,0:T(8,128)(2,1)}, bf16[2,256,768]{2,1,0:T(8,128)(2,1)}, u32[]{:S(2)}, u32[]{:S(2)}) collective-permute-start(bf16[2,256,768]{2,1,0:T(8,128)(2,1)} %collective-permute-done.3.refs_4_), channel_id=1, source_target_pairs={{0,252},{4,0},{8,4},{12,8},{16,12},{20,16},{24,20},{28,24},{32,28}... | collective-permute-start | bytes 2359304 | tf_op jit(solution)/shard_map/ppermute | solution.py:19
  123.1 58.5 %copy-start.1 = (bf16[256,768]{1,0:T(8,128)(2,1)S(1)}, bf16[256,768]{1,0:T(8,128)(2,1)}, u32[]{:S(2)}) copy-start(bf16[256,768]{1,0:T(8,128)(2,1)} %param.11) | copy-start | bytes 1179652
  123.1 58.5 %copy-start.2 = (bf16[256,768]{1,0:T(8,128)(2,1)S(1)}, bf16[256,768]{1,0:T(8,128)(2,1)}, u32[]{:S(2)}) copy-start(bf16[256,768]{1,0:T(8,128)(2,1)} %shard_map.91) | copy-start | bytes 1179652
  124.2 59.2 %copy-start.6 = (f32[768]{0:T(1024)S(1)}, f32[768]{0:T(1024)}, u32[]{:S(2)}) copy-start(f32[768]{0:T(1024)} %param.15) | copy-start | bytes 9220
Sparse Core Ops, SparseCore 0:
  9.5 50.1 all-gather.2

commit v2 on v1

--- a/solution.py
+++ b/solution.py
@@ -96,8 +96,8 @@
     )(mask, q, *blocks)
 
 
-def spread_kernel(x_size, up_z, down_z, out_z, up_full, down_full, out_full,
-                  send_sems, recv_sems, local_sems):
+def spread_kernel(x_size, kv, up_z, down_z, out_z, kv_out, up_full, down_full, out_full,
+                  send_sems, recv_sems, local_sems, kv_send, kv_recv):
     blk = lax.axis_index("blk")
     head = lax.axis_index("head")
     bend = lax.axis_index("bend")
@@ -106,6 +106,11 @@
     left = (hi * x_size + (x + x_size - 1) % x_size, head, bend)
     right = (hi * x_size + (x + 1) % x_size, head, bend)
     partner = (blk, head, bend + 1 - 2 * c)
+    n_head = lax.axis_size("head")
+    n_ring = lax.axis_size("blk") * n_head
+    me = blk * n_head + head
+    ring_right = ((me + 1) % n_ring // n_head, (me + 1) % n_head, bend)
+    ring_left = ((me + n_ring - 1) % n_ring // n_head, (me + n_ring - 1) % n_head, bend)
     p_own = x * 2 + c
     p_left = ((x + x_size - 1) % x_size) * 2 + c
     p_right = ((x + 1) % x_size) * 2 + c
@@ -115,9 +120,18 @@
     heads = down_z.shape[0]
 
     barrier = pltpu.get_barrier_semaphore()
-    for dev in (left, right, partner):
+    for dev in (left, right, partner, ring_left, ring_right):
         pl.semaphore_signal(barrier, inc=1, device_id=dev, device_id_type=MESH)
-    pl.semaphore_wait(barrier, 3)
+    pl.semaphore_wait(barrier, 5)
+
+    def kv_send_to(src, slot, dev):
+        copy = pltpu.make_async_remote_copy(
+            src_ref=src, dst_ref=kv_out.at[slot], send_sem=kv_send.at[slot],
+            recv_sem=kv_recv.at[slot], device_id=dev, device_id_type=MESH)
+        copy.start()
+        return copy
+
+    kv_sent = [kv_send_to(kv, 0, ring_right), kv_send_to(kv, 1, ring_left)]
 
     def up_at(p, part=None):
         cols = pl.ds(pl.multiple_of(p * width, 128), width)
@@ -154,6 +168,9 @@
         send(up_z, up_at(p_own), 5, partner),
         send(down_z, down_at(p_own), 6, partner),
     ]
+    kv_sent[0].wait_recv()
+    kv_sent[1].wait_recv()
+    kv_sent += [kv_send_to(kv_out.at[0], 2, ring_right), kv_send_to(kv_out.at[1], 3, ring_left)]
     a_up_r.wait_recv()
     a_dn_r.wait_recv()
     b_up_r = send(up_at(p_left, 0), up_at(p_left, 0), 7, right)
@@ -168,6 +185,9 @@
     sent += [b_up_l, b_dn_l]
     sent += [send(up_at(p_right), up_at(p_right), 13, partner),
              send(down_at(p_right), down_at(p_right), 14, partner)]
+    kv_sent[2].wait_recv()
+    kv_sent[3].wait_recv()
+    kv_sent += [kv_send_to(kv_out.at[2], 4, ring_right), kv_send_to(kv_out.at[3], 5, ring_left)]
     b_up_r.wait_recv()
     b_dn_r.wait_recv()
     sent += [send(up_at(p_far, 0), up_at(p_far, 0), 15, partner),
@@ -178,13 +198,15 @@
              send(down_at(p_far, 1), down_at(p_far, 1), 18, partner)]
     for k in (4, 5, 6, 9, 10, 13, 14, 15, 16, 17, 18):
         sent[k].wait_recv()
-    for copy in sent:
+    kv_sent[4].wait_recv()
+    kv_sent[5].wait_recv()
+    for copy in sent + kv_sent:
         copy.wait_send()
     for copy in local:
         copy.wait()
 
 
-def spread_weights(up_z, down_z, out_z, x_size):
+def exchange(kv, up_z, down_z, out_z, x_size):
     rows, width = up_z.shape
     heads, down_rows, d = down_z.shape
     n_pieces = 2 * x_size
@@ -192,19 +214,22 @@
     return pl.pallas_call(
         functools.partial(spread_kernel, x_size),
         out_shape=(
+            jax.ShapeDtypeStruct((2 * REACH,) + kv.shape, kv.dtype),
             jax.ShapeDtypeStruct((rows, n_pieces * width), up_z.dtype),
             jax.ShapeDtypeStruct((heads, n_pieces, down_rows, d), down_z.dtype),
             jax.ShapeDtypeStruct((heads, 2) + out_z.shape[1:], out_z.dtype),
         ),
-        in_specs=[any_spec] * 3,
-        out_specs=(any_spec, any_spec, any_spec),
+        in_specs=[any_spec] * 4,
+        out_specs=(any_spec, any_spec, any_spec, any_spec),
         scratch_shapes=[
             pltpu.SemaphoreType.DMA((19,)),
             pltpu.SemaphoreType.DMA((19,)),
             pltpu.SemaphoreType.DMA((3,)),
+            pltpu.SemaphoreType.DMA((2 * REACH,)),
+            pltpu.SemaphoreType.DMA((2 * REACH,)),
         ],
         compiler_params=pltpu.CompilerParams(collective_id=1, has_side_effects=True),
-    )(up_z, down_z, out_z)
+    )(kv, up_z, down_z, out_z)
 
 
 def shards(
@@ -246,18 +271,15 @@
     out_z = by_head[:, :o0].reshape(n_heads, out_rows, d)
     up_z = by_head[:, o0:o1].reshape(-1, up_cols)
     down_z = by_head[:, o1:].reshape(n_heads, down_rows, d)
-    up_full, down_full, out_full = spread_weights(up_z, down_z, out_z, x_size)
+    near, up_full, down_full, out_full = exchange(keys_values, up_z, down_z, out_z, x_size)
     out_full = out_full.reshape(d, d)
     down_full = down_full.reshape(-1, d)
 
     blocks = [keys_values]
     ids = [own_index]
-    left = right = keys_values
-    for d in range(1, REACH + 1):
-        left = ring_shift(left, ("blk", "head"), loop_size, 1)
-        right = ring_shift(right, ("blk", "head"), loop_size, -1)
-        blocks += [left, right]
-        ids += [(own_index - d) % loop_size, (own_index + d) % loop_size]
+    for dist in range(1, REACH + 1):
+        blocks += [near[2 * dist - 2], near[2 * dist - 1]]
+        ids += [(own_index - dist) % loop_size, (own_index + dist) % loop_size]
     entry_live = jnp.arange(LIST, dtype=jnp.int32) < list_lengths[0]
     mask = jnp.stack(
         [jnp.any((block_lists[0] == b) & entry_live) for b in ids]).astype(jnp.int32)

time: 201 us -> 202 us (level)
  Pallas kernels: 78.6 us -> 121 us
  starting transfers between devices: 25.8 us -> 0.01 us
  waiting for transfers between devices: 53.9 us -> 36.3 us
  local copies, waits for them, and re-layouts: 13.3 us -> 17.7 us
    ppermute x6 -> x0, waiting for transfers between devices: 53.9 us -> none  [ring_shift(): return lax.ppermute(block, axis, route)]
    pallas_call x1, Pallas kernels: 55.1 us -> 97 us  [exchange(): pl.pallas_call(functools.partial(spread_kernel, x_size), out_shape=(jax.S...]
    all_gather x1, waiting for transfers between devices: 0.01 us -> 36.3 us  [shards(): by_head = lax.all_gather(packed, 'head', axis=0, tiled=False)]
    ppermute x6 -> x0, starting transfers between devices: 25.8 us -> none  [ring_shift(): return lax.ppermute(block, axis, route)]
    squeeze x0 -> x1, local copies, waits for them, and re-layouts: none -> 4.53 us  [shards(): blocks += [near[2 * dist - 2], near[2 * dist - 1]]]
  transfers between devices with their start and end apart: 7 -> 1, of which waited for: 4 -> 1; matrix products, arithmetic and copies ran while one was open for 3% -> 3% of each run, Pallas kernels for 12% -> 0%
where the time goes in v2:
time: 202 us; the launch traced here: 201 us
  Pallas kernels  121 us (60%)
  waiting for transfers between devices  36.3 us (18%)
  local copies, waits for them, and re-layouts  17.7 us (9%)
  between operations  14.2 us (7%)
  matrix products  9.08 us (4%)
  other arithmetic  2.72 us (1%)
    pallas_call x1, Pallas kernels, exchange(): pl.pallas_call(functools.partial(spread_kernel, x_size), out_shape=(jax.S...  97 us
    all_gather x1, waiting for transfers between devices, shards(): by_head = lax.all_gather(packed, 'head', axis=0, tiled=False)  36.3 us
    pallas_call x1, Pallas kernels, attend(): pl.pallas_call(functools.partial(attention_kernel, n_blocks), grid_spec=g...  23.6 us
    dot_general x1, matrix products, shards(): jnp.dot(activated, down_full, preferred_element_type=jnp.float32)  7.52 us
    another operation x1, local copies, waits for them, and re-layouts, shards(): jnp.stack([jnp.any((block_lists[0] == b) & entry_live) for b in ids])  4.54 us
    squeeze x1, local copies, waits for them, and re-layouts, shards(): blocks += [near[2 * dist - 2], near[2 * dist - 1]]  4.53 us
  transfers between devices with their start and end apart: 1, of which 1 were waited for; matrix products, arithmetic and copies ran while one was open for 3% of the time, Pallas kernels for 0%

profile of v2, /device:TPU:8, one launch (start us, length us, event | category | flops | bytes accessed | tf_op | source)
XLA Modules:
  0.0 200.6 jit_solution(7538166237300447197)
XLA Ops:
  6.5 0.0 copy-start
  6.5 0.0 all-gather.3.cloned.1.call-start
  6.5 1.0 constant_dynamic-slice_fusion.2
  7.5 0.1 reshape.47
  7.6 0.1 copy-done
  7.7 0.9 constant_dynamic-slice_fusion
  8.6 0.1 reshape.49
  8.7 0.7 pad_maximum_fusion
  9.4 0.0 all-gather.3.cloned.1.call-update
  10.1 1.5 fusion.25
  11.6 4.5 %stack.31 = pred[7]{0:T(512)(128)(4,1)S(1)} concatenate(pred[1]{0:T(512)(128)(4,1)} %bitcast.2, pred[1]{0:T(512)(128)(4,1)} %bitcast.4, pred[1]{0:T(512)(128)(4,1)} %bitcast.6, pred[1]{0:T(512)(128)(4,1)} %bitcast.8, pred[1]{0:T(512)(128)(4,1)} %bitcast.10, pred[1]{0:T(512)(128)(4,1)} %bitcast.12, pred[1]{0:T(512)(128)(4,1)} %bitcast.14), dimensions={0} | concatenate | bytes 14 | tf_op jit(solution)/shard_map/stack | solution.py:284
  16.1 0.5 convert_element_type.16.mask_ref
  16.7 36.3 %all-gather.3.cloned.1.call-done = bf16[884736]{0:T(1024)(128)(2,1)} async-done(((bf16[110592]{0:T(1024)(128)(2,1)}), bf16[884736]{0:T(1024)(128)(2,1)}) %all-gather.3.cloned.1.call-update) | async-done | bytes 1769488 | tf_op jit(solution)/shard_map/all_gather | solution.py:267
  52.9 2.2 %reshape.55 = bf16[8,110592]{1,0:T(8,128)(2,1)S(1)} reshape(bf16[884736]{0:T(1024)(128)(2,1)} %all-gather.3.cloned.1.call-done) | data formatting | bytes 3538944 | tf_op jit(solution)/shard_map/all_gather | solution.py:267
  55.1 0.9 fusion.36
  56.1 1.1 reshape.50.up_z
  57.2 2.3 %copy_bitcast_fusion = (bf16[8,48,768]{2,1,0:T(8,128)(2,1)}, bf16[8,48,768]{2,1,0:T(8,128)(2,1)}) fusion(bf16[1,8,48,768]{3,1,2,0:T(8,128)(2,1)S(1)} %bitcast.61, bf16[1,8,48,768]{3,1,2,0:T(8,128)(2,1)} %bitcast.62), kind=kLoop, calls=%fused_computation.25 | loop fusion | bytes 2359296 | tf_op jit(solution)/shard_map/reshape | solution.py:271
  59.5 97.0 %shard_map.91 = (bf16[6,2,256,768]{3,2,1,0:T(8,128)(2,1)}, bf16[768,3072]{1,0:T(8,128)(2,1)}, bf16[8,8,48,768]{3,2,1,0:T(8,128)(2,1)}, bf16[8,2,48,768]{3,2,1,0:T(8,128)(2,1)}) custom-call(bf16[2,256,768]{2,1,0:T(8,128)(2,1)} %refs_0_.1, bf16[768,384]{1,0:T(8,128)(2,1)} %reshape.50.up_z, bf16[8,48,768]{2,1,0:T(8,128)(2,1)} %get-tuple-element.32.down_z, ...), custom_call_target="tpu_custom_call" | custom-call | tf_op jit(solution)/shard_map/pallas_call | solution.py:214
  156.5 4.5 %slice_bitcast_fusion = (bf16[2,256,768]{2,1,0:T(8,128)(2,1)}, bf16[2,256,768]{2,1,0:T(8,128)(2,1)}, bf16[2,256,768]{2,1,0:T(8,128)(2,1)}, bf16[2,256,768]{2,1,0...) fusion(bf16[6,2,256,768]{3,2,1,0:T(8,128)(2,1)} %get-tuple-element.9), kind=kLoop, calls=%fused_computation.19 | loop fusion | bytes 9437184 | tf_op jit(solution)/shard_map/squeeze | solution.py:281
  161.0 0.0 copy-start.1
  161.0 0.0 copy-start.2
  161.0 0.0 copy-start.3
  161.0 23.6 %shard_map.92 = bf16[256,768]{1,0:T(8,128)(2,1)} custom-call(s32[7]{0:T(128)} %convert_element_type.16.mask_ref, bf16[256,768]{1,0:T(8,128)(2,1)} %q_ref.1, bf16[2,256,768]{2,1,0:T(8,128)(2,1)} %refs_0_.1, bf16[2,256,768]{2,1,0:T(8,128)(2,1)} %get-tuple-element.25.refs_1_, bf16[2,256,768]{2,1,0:T(8,128)(2,1)} %get-tuple-element.24.refs_2_, ...), custom_call_target="tpu_custom_call" | custom-call | flops 2415919104 | bytes 6291456 | tf_op jit(solution)/shard_map/pallas_call | solution.py:87
  184.7 0.0 copy-done.1
  184.7 0.0 copy-done.2
  184.7 1.6 multiply_reduce_fusion
  186.3 0.0 copy-done.3
  186.3 7.5 %fusion.17 = bf16[256,768]{1,0:T(8,128)(2,1)} fusion(f32[256,768]{1,0:T(8,128)S(1)} %get-tuple-element.30, bf16[3072,768]{1,0:T(8,128)(2,1)} %bitcast.64, bf16[768,3072]{1,0:T(8,128)(2,1)} %get-tuple-element.11, f32[768]{0:T(1024)S(1)} %copy-done.3, f32[256]{0:T(256)S(1)} %add_rsqrt_fusion), kind=kOutput, calls=%fused_computation.16 | convolution fusion | flops 2423980032 | bytes 10620928 | tf_op jit(solution)/shard_map/dot_general | solution.py:294
  (3 shorter events, 0.1 us)
Async XLA Ops:
  6.5 1.1 copy-start
  6.5 46.4 %all-gather.3.cloned.1.call-start = ((), (), s32[]{:S(2)}) async-start(), calls=%async_computation | async-start | bytes 1990656 | tf_op jit(solution)/shard_map/all_gather | solution.py:267
  161.0 23.6 %copy-start.1 = (bf16[8,2,48,768]{3,2,1,0:T(8,128)(2,1)S(1)}, bf16[8,2,48,768]{3,2,1,0:T(8,128)(2,1)}, u32[]{:S(2)}) copy-start(bf16[8,2,48,768]{3,2,1,0:T(8,128)(2,1)} %get-tuple-element.10) | copy-start | bytes 3538948
  161.0 23.6 %copy-start.2 = (bf16[256,768]{1,0:T(8,128)(2,1)S(1)}, bf16[256,768]{1,0:T(8,128)(2,1)}, u32[]{:S(2)}) copy-start(bf16[256,768]{1,0:T(8,128)(2,1)} %param.11) | copy-start | bytes 1179652
  161.0 25.2 %copy-start.3 = (f32[768]{0:T(1024)S(1)}, f32[768]{0:T(1024)}, u32[]{:S(2)}) copy-start(f32[768]{0:T(1024)} %param.15) | copy-start | bytes 9220
Sparse Core Ops, SparseCore 0:
  9.5 43.3 all-gather.2

commit v3 on v2

--- a/solution.py
+++ b/solution.py
@@ -96,7 +96,9 @@
     )(mask, q, *blocks)
 
 
-def spread_kernel(x_size, kv, up_z, down_z, out_z, kv_out, up_full, down_full, out_full,
+def spread_kernel(x_size, bias_ref, q_ref, kv, up_z, down_z, out_z,
+                  ctx_ref, up_full, down_full, out_full,
+                  slots, q_t, m_scr, l_scr, acc_scr,
                   send_sems, recv_sems, local_sems, kv_send, kv_recv):
     blk = lax.axis_index("blk")
     head = lax.axis_index("head")
@@ -118,6 +120,9 @@
     width = up_z.shape[1]
     rows = up_z.shape[0]
     heads = down_z.shape[0]
+    pair = 2 * HD
+    n_pairs = q_ref.shape[1] // pair
+    scale = 1.0 / HD**0.5
 
     barrier = pltpu.get_barrier_semaphore()
     for dev in (left, right, partner, ring_left, ring_right):
@@ -126,12 +131,10 @@
 
     def kv_send_to(src, slot, dev):
         copy = pltpu.make_async_remote_copy(
-            src_ref=src, dst_ref=kv_out.at[slot], send_sem=kv_send.at[slot],
+            src_ref=src, dst_ref=slots.at[slot], send_sem=kv_send.at[slot],
             recv_sem=kv_recv.at[slot], device_id=dev, device_id_type=MESH)
         copy.start()
         return copy
-
-    kv_sent = [kv_send_to(kv, 0, ring_right), kv_send_to(kv, 1, ring_left)]
 
     def up_at(p, part=None):
         cols = pl.ds(pl.multiple_of(p * width, 128), width)
@@ -151,6 +154,7 @@
         copy.start()
         return copy
 
+    kv_sent = [kv_send_to(kv, 0, ring_right), kv_send_to(kv, 1, ring_left)]
     local = [
         pltpu.make_async_copy(up_z, up_at(p_own), local_sems.at[0]),
         pltpu.make_async_copy(down_z, down_at(p_own), local_sems.at[1]),
@@ -168,9 +172,40 @@
         send(up_z, up_at(p_own), 5, partner),
         send(down_z, down_at(p_own), 6, partner),
     ]
+
+    first = lax.broadcasted_iota(jnp.int32, (pair, q_ref.shape[0]), 0) < HD
+    for p in range(n_pairs):
+        qp = q_ref[:, p * pair:(p + 1) * pair].T
+        q_t[2 * p] = jnp.where(first, qp, jnp.zeros_like(qp))
+        q_t[2 * p + 1] = jnp.where(first, jnp.zeros_like(qp), qp)
+    m_scr[...] = jnp.full(m_scr.shape, -jnp.inf, jnp.float32)
+    l_scr[...] = jnp.zeros(l_scr.shape, jnp.float32)
+    acc_scr[...] = jnp.zeros(acc_scr.shape, jnp.float32)
+
+    def absorb(block, bias):
+        def one_pair(p, carry):
+            cols = pl.ds(pl.multiple_of(p * pair, pair), pair)
+            k = block[0, :, cols]
+            v_t = block[1, :, cols].T
+            for hh in range(2):
+                h = 2 * p + hh
+                s_t = jnp.dot(k, q_t[h], preferred_element_type=jnp.float32) * scale + bias
+                m_old = m_scr[h]
+                m_new = jnp.maximum(m_old, jnp.max(s_t, axis=0, keepdims=True))
+                alpha = jnp.exp(m_old - m_new)
+                w_t = jnp.exp(s_t - m_new)
+                l_scr[h] = alpha * l_scr[h] + jnp.sum(w_t, axis=0, keepdims=True)
+                acc_scr[h] = alpha * acc_scr[h] + jnp.dot(
+                    v_t, w_t.astype(jnp.bfloat16), preferred_element_type=jnp.float32)
+                m_scr[h] = m_new
+            return carry
+        lax.fori_loop(0, n_pairs, one_pair, 0)
+
+    absorb(kv, bias_ref[0])
+
     kv_sent[0].wait_recv()
     kv_sent[1].wait_recv()
-    kv_sent += [kv_send_to(kv_out.at[0], 2, ring_right), kv_send_to(kv_out.at[1], 3, ring_left)]
+    kv_sent += [kv_send_to(slots.at[0], 2, ring_right), kv_send_to(slots.at[1], 3, ring_left)]
     a_up_r.wait_recv()
     a_dn_r.wait_recv()
     b_up_r = send(up_at(p_left, 0), up_at(p_left, 0), 7, right)
@@ -185,9 +220,13 @@
     sent += [b_up_l, b_dn_l]
     sent += [send(up_at(p_right), up_at(p_right), 13, partner),
              send(down_at(p_right), down_at(p_right), 14, partner)]
+
+    absorb(slots.at[0], bias_ref[1])
+    absorb(slots.at[1], bias_ref[2])
+
     kv_sent[2].wait_recv()
     kv_sent[3].wait_recv()
-    kv_sent += [kv_send_to(kv_out.at[2], 4, ring_right), kv_send_to(kv_out.at[3], 5, ring_left)]
+    kv_sent += [kv_send_to(slots.at[2], 4, ring_right), kv_send_to(slots.at[3], 5, ring_left)]
     b_up_r.wait_recv()
     b_dn_r.wait_recv()
     sent += [send(up_at(p_far, 0), up_at(p_far, 0), 15, partner),
@@ -196,40 +235,69 @@
     b_dn_l.wait_recv()
     sent += [send(up_at(p_far, 1), up_at(p_far, 1), 17, partner),
              send(down_at(p_far, 1), down_at(p_far, 1), 18, partner)]
+
+    absorb(slots.at[2], bias_ref[3])
+    absorb(slots.at[3], bias_ref[4])
+
+    kv_sent[4].wait_recv()
+    kv_sent[5].wait_recv()
+    absorb(slots.at[4], bias_ref[5])
+    absorb(slots.at[5], bias_ref[6])
+
+    row = lax.broadcasted_iota(jnp.int32, (pair, q_ref.shape[0]), 0) < HD
+
+    def write_pair(p, carry):
+        out_t = jnp.where(row, acc_scr[2 * p] / l_scr[2 * p], acc_scr[2 * p + 1] / l_scr[2 * p + 1])
+        ctx_ref[:, pl.ds(pl.multiple_of(p * pair, pair), pair)] = out_t.T.astype(ctx_ref.dtype)
+        return carry
+    lax.fori_loop(0, n_pairs, write_pair, 0)
+
     for k in (4, 5, 6, 9, 10, 13, 14, 15, 16, 17, 18):
         sent[k].wait_recv()
-    kv_sent[4].wait_recv()
-    kv_sent[5].wait_recv()
     for copy in sent + kv_sent:
         copy.wait_send()
     for copy in local:
         copy.wait()
 
 
-def exchange(kv, up_z, down_z, out_z, x_size):
+def exchange(bias, q, kv, up_z, down_z, out_z, x_size):
     rows, width = up_z.shape
     heads, down_rows, d = down_z.shape
+    n_rows = q.shape[0]
     n_pieces = 2 * x_size
     any_spec = pl.BlockSpec(memory_space=pl.ANY)
+    vmem_spec = pl.BlockSpec(memory_space=pltpu.VMEM)
     return pl.pallas_call(
         functools.partial(spread_kernel, x_size),
         out_shape=(
-            jax.ShapeDtypeStruct((2 * REACH,) + kv.shape, kv.dtype),
+            jax.ShapeDtypeStruct(q.shape, jnp.bfloat16),
             jax.ShapeDtypeStruct((rows, n_pieces * width), up_z.dtype),
             jax.ShapeDtypeStruct((heads, n_pieces, down_rows, d), down_z.dtype),
             jax.ShapeDtypeStruct((heads, 2) + out_z.shape[1:], out_z.dtype),
         ),
-        in_specs=[any_spec] * 4,
-        out_specs=(any_spec, any_spec, any_spec, any_spec),
+        in_specs=[pl.BlockSpec(memory_space=pltpu.SMEM), vmem_spec, vmem_spec,
+                  any_spec, any_spec, any_spec],
+        out_specs=(vmem_spec, any_spec, any_spec, any_spec),
         scratch_shapes=[
+            pltpu.VMEM((2 * REACH,) + kv.shape, kv.dtype),
+            pltpu.VMEM((HEADS, 2 * HD, n_rows), jnp.bfloat16),
+            pltpu.VMEM((HEADS, 1, n_rows), jnp.float32),
+            pltpu.VMEM((HEADS, 1, n_rows), jnp.float32),
+            pltpu.VMEM((HEADS, 2 * HD, n_rows), jnp.float32),
             pltpu.SemaphoreType.DMA((19,)),
             pltpu.SemaphoreType.DMA((19,)),
             pltpu.SemaphoreType.DMA((3,)),
             pltpu.SemaphoreType.DMA((2 * REACH,)),
             pltpu.SemaphoreType.DMA((2 * REACH,)),
         ],
-        compiler_params=pltpu.CompilerParams(collective_id=1, has_side_effects=True),
-    )(kv, up_z, down_z, out_z)
+        compiler_params=pltpu.CompilerParams(
+            collective_id=1, has_side_effects=True, vmem_limit_bytes=48 * 1024 * 1024),
+        cost_estimate=pl.CostEstimate(
+            flops=6 * n_rows * n_rows * q.shape[1] * (2 * REACH + 1),
+            transcendentals=n_rows * n_rows * HEADS * (2 * REACH + 1),
+            bytes_accessed=2 * (rows * n_pieces * width + heads * n_pieces * down_rows * d),
+        ),
+    )(bias, q, kv, up_z, down_z, out_z)
 
 
 def shards(
@@ -271,19 +339,16 @@
     out_z = by_head[:, :o0].reshape(n_heads, out_rows, d)
     up_z = by_head[:, o0:o1].reshape(-1, up_cols)
     down_z = by_head[:, o1:].reshape(n_heads, down_rows, d)
-    near, up_full, down_full, out_full = exchange(keys_values, up_z, down_z, out_z, x_size)
+    ids = [own_index]
+    for dist in range(1, REACH + 1):
+        ids += [(own_index - dist) % loop_size, (own_index + dist) % loop_size]
+    entry_live = jnp.arange(LIST, dtype=jnp.int32) < list_lengths[0]
+    listed = jnp.stack([jnp.any((block_lists[0] == b) & entry_live) for b in ids])
+    bias = jnp.where(listed, 0.0, -1e30).astype(jnp.float32)
+    context, up_full, down_full, out_full = exchange(
+        bias, queries, keys_values, up_z, down_z, out_z, x_size)
     out_full = out_full.reshape(d, d)
     down_full = down_full.reshape(-1, d)
-
-    blocks = [keys_values]
-    ids = [own_index]
-    for dist in range(1, REACH + 1):
-        blocks += [near[2 * dist - 2], near[2 * dist - 1]]
-        ids += [(own_index - dist) % loop_size, (own_index + dist) % loop_size]
-    entry_live = jnp.arange(LIST, dtype=jnp.int32) < list_lengths[0]
-    mask = jnp.stack(
-        [jnp.any((block_lists[0] == b) & entry_live) for b in ids]).astype(jnp.int32)
-    context = attend(mask, queries, blocks)
 
     hidden = surface.astype(jnp.float32) + jnp.dot(
         context, out_full, preferred_element_type=jnp.float32)

time: 202 us -> 187 us (0.926)
  Pallas kernels: 121 us -> 112 us
  local copies, waits for them, and re-layouts: 17.7 us -> 12.9 us
    pallas_call x1 -> x0, Pallas kernels: 23.6 us -> none  [attend(): pl.pallas_call(functools.partial(attention_kernel, n_blocks), grid_spec=g...]
    pallas_call x1, Pallas kernels: 97 us -> 112 us  [exchange(): pl.pallas_call(functools.partial(spread_kernel, x_size), out_shape=(jax.S...]
    squeeze x1 -> x0, local copies, waits for them, and re-layouts: 4.53 us -> none  [shards(): blocks += [near[2 * dist - 2], near[2 * dist - 1]]]
where the time goes in v3:
time: 187 us; the launch traced here: 186 us
  Pallas kernels  112 us (60%)
  waiting for transfers between devices  36.8 us (20%)
  between operations  14.2 us (8%)
  local copies, waits for them, and re-layouts  12.9 us (7%)
  matrix products  8.09 us (4%)
  other arithmetic  2.18 us (1%)
    pallas_call x1, Pallas kernels, exchange(): pl.pallas_call(functools.partial(spread_kernel, x_size), out_shape=(jax.S...  112 us
    all_gather x1, waiting for transfers between devices, shards(): by_head = lax.all_gather(packed, 'head', axis=0, tiled=False)  36.8 us
    dot_general x1, matrix products, shards(): jnp.dot(activated, down_full, preferred_element_type=jnp.float32)  7.52 us
    another operation x1, local copies, waits for them, and re-layouts, shards(): jnp.stack([jnp.any((block_lists[0] == b) & entry_live) for b in ids])  4.54 us
  transfers between devices with their start and end apart: 1, of which 1 were waited for; matrix products, arithmetic and copies ran while one was open for 3% of the time, Pallas kernels for 0%

profile of v3, /device:TPU:8, one launch (start us, length us, event | category | flops | bytes accessed | tf_op | source)
XLA Modules:
  0.0 186.4 jit_solution(10768496360484512688)
XLA Ops:
  6.5 0.0 copy-start
  6.5 0.0 all-gather.3.cloned.1.call-start
  6.5 1.0 constant_dynamic-slice_fusion.2
  7.5 0.1 reshape.47
  7.6 0.1 copy-done
  7.7 0.9 constant_dynamic-slice_fusion
  8.6 0.1 reshape.49
  8.7 0.7 pad_maximum_fusion
  9.4 0.0 all-gather.3.cloned.1.call-update
  10.1 1.5 fusion.25
  11.6 4.5 %stack.31 = pred[7]{0:T(512)(128)(4,1)S(1)} concatenate(pred[1]{0:T(512)(128)(4,1)} %bitcast.2, pred[1]{0:T(512)(128)(4,1)} %bitcast.4, pred[1]{0:T(512)(128)(4,1)} %bitcast.6, pred[1]{0:T(512)(128)(4,1)} %bitcast.8, pred[1]{0:T(512)(128)(4,1)} %bitcast.10, pred[1]{0:T(512)(128)(4,1)} %bitcast.12, pred[1]{0:T(512)(128)(4,1)} %bitcast.14), dimensions={0} | concatenate | bytes 14 | tf_op jit(solution)/shard_map/stack | solution.py:346
  16.1 36.8 %all-gather.3.cloned.1.call-done = bf16[884736]{0:T(1024)(128)(2,1)} async-done(((bf16[110592]{0:T(1024)(128)(2,1)}), bf16[884736]{0:T(1024)(128)(2,1)}) %all-gather.3.cloned.1.call-update) | async-done | bytes 1769488 | tf_op jit(solution)/shard_map/all_gather | solution.py:335
  52.9 2.2 %reshape.55 = bf16[8,110592]{1,0:T(8,128)(2,1)S(1)} reshape(bf16[884736]{0:T(1024)(128)(2,1)} %all-gather.3.cloned.1.call-done) | data formatting | bytes 3538944 | tf_op jit(solution)/shard_map/all_gather | solution.py:335
  55.1 0.0 copy-start.1
  55.2 0.0 copy-start.2
  55.2 1.3 fusion.36
  56.4 1.3 reshape.50.up_z
  57.8 1.5 copy_bitcast_fusion
  59.2 0.0 copy-done.1
  59.2 0.0 copy-done.2
  59.2 0.0 copy-start.3
  59.3 0.0 copy-start.4
  59.3 112.1 %shard_map.91 = (bf16[256,768]{1,0:T(8,128)(2,1)S(1)}, bf16[768,3072]{1,0:T(8,128)(2,1)}, bf16[8,8,48,768]{3,2,1,0:T(8,128)(2,1)}, bf16[8,2,48,768]{3,2,1,0:T(8,128)(2,1)S(1)}) custom-call(f32[7]{0:T(128)S(1)} %broadcast_select_fusion.bias_ref, bf16[256,768]{1,0:T(8,128)(2,1)S(1)} %copy-done.2, bf16[2,256,768]{2,1,0:T(8,128)(2,1)S(1)} %copy-done.1, ...), custom_call_target="tpu_custom_call" | custom-call | flops 2113929216 | bytes 9437184 | tf_op jit(solution)/shard_map/pallas_call | solution.py:270
  171.4 0.0 copy-done.3
  171.4 0.6 multiply_reduce_fusion
  172.0 0.0 copy-done.4
  172.0 7.5 %fusion.17 = bf16[256,768]{1,0:T(8,128)(2,1)} fusion(f32[256,768]{1,0:T(8,128)S(1)} %get-tuple-element.24, bf16[3072,768]{1,0:T(8,128)(2,1)} %bitcast.52, bf16[768,3072]{1,0:T(8,128)(2,1)} %get-tuple-element.11, f32[768]{0:T(1024)S(1)} %copy-done.4, f32[256]{0:T(256)S(1)} %add_rsqrt_fusion), kind=kOutput, calls=%fused_computation.16 | convolution fusion | flops 2423980032 | bytes 10620928 | tf_op jit(solution)/shard_map/dot_general | solution.py:359
  (4 shorter events, 0.1 us)
Async XLA Ops:
  6.5 1.1 copy-start
  6.5 46.4 %all-gather.3.cloned.1.call-start = ((), (), s32[]{:S(2)}) async-start(), calls=%async_computation | async-start | bytes 1990656 | tf_op jit(solution)/shard_map/all_gather | solution.py:335
  55.1 4.1 %copy-start.1 = (bf16[2,256,768]{2,1,0:T(8,128)(2,1)S(1)}, bf16[2,256,768]{2,1,0:T(8,128)(2,1)}, u32[]{:S(2)}) copy-start(bf16[2,256,768]{2,1,0:T(8,128)(2,1)} %kv.1) | copy-start | bytes 2359300
  55.2 4.1 %copy-start.2 = (bf16[256,768]{1,0:T(8,128)(2,1)S(1)}, bf16[256,768]{1,0:T(8,128)(2,1)}, u32[]{:S(2)}) copy-start(bf16[256,768]{1,0:T(8,128)(2,1)} %q_ref.1) | copy-start | bytes 1179652
  59.2 112.2 %copy-start.3 = (bf16[256,768]{1,0:T(8,128)(2,1)S(1)}, bf16[256,768]{1,0:T(8,128)(2,1)}, u32[]{:S(2)}) copy-start(bf16[256,768]{1,0:T(8,128)(2,1)} %param.11) | copy-start | bytes 1179652
  59.3 112.7 %copy-start.4 = (f32[768]{0:T(1024)S(1)}, f32[768]{0:T(1024)}, u32[]{:S(2)}) copy-start(f32[768]{0:T(1024)} %param.15) | copy-start | bytes 9220
Sparse Core Ops, SparseCore 0:
  9.5 43.3 all-gather.2
